TPU v7x, 32 devices: a whole 2x2x4 slice. The times are simulated.
32 devices in a mesh: vol: 2 (over y), gz: 16 (over z, x, core).
Axes of the slice: x: 2, y: 2, z: 4, core: 2. Of those that a mesh axis runs over, the one named last changes fastest.
Arguments:
- volume: bfloat16 [2, 32, 64, 64, 128], P('vol', None, 'gz'), may hold values from -6 to 6
- kernel: bfloat16 [64, 32, 3, 3, 3], replicated, may hold values from -0.21875 to 0.21875
- cotangent: bfloat16 [2, 64, 32, 32, 64], P('vol', None, None, 'gz'), may hold values from -6 to 6
Outputs:
- features: bfloat16 [2, 64, 32, 32, 64], P('vol', None, None, 'gz')
- volume_grad: bfloat16 [2, 32, 64, 64, 128], P('vol', None, 'gz')
- kernel_grad: float32 [64, 32, 3, 3, 3], replicated
All inputs are finite; a program needn't handle non-finite values.
Results may differ from a plain program's by a relative error of at most 0.004.
Values may be sent and summed in bfloat16 or wider, within the bound.
No kernel may reach another device: no remote copies, remote signals or barrier semaphores. Data moves between devices by JAX's collectives and lax.ppermute only.
A program may use at most 192 MiB of HBM per device.

v0:
```python
import jax
import jax.numpy as jnp
from jax import lax
from jax.experimental import pallas as pl
from jax.experimental.pallas import tpu as pltpu
from jax.sharding import PartitionSpec as P

F32 = jnp.float32
BF16 = jnp.bfloat16
TAP = {(0, 0): 1, (0, 1): 2, (1, 1): 0, (1, 0): None}


def dot(a, b):
    return lax.dot_general(a, b, (((1,), (0,)), ((), ())), preferred_element_type=F32)


def dot_t(a, b):
    return lax.dot_general(a, b, (((1,), (1,)), ((), ())), preferred_element_type=F32)


def iota(shape, dim):
    return lax.broadcasted_iota(jnp.int32, shape, dim)


def split_matrix(x, swapped):
    shape = (2 * x, 2 * x)
    row, col = iota(shape, 0), iota(shape, 1)
    half_in, x_in = row // x, row % x
    parity, half_out, r = col // x, (col % x) // (x // 2), col % (x // 2)
    if swapped:
        half_out = 1 - half_out
    hit = (half_in == half_out) & (x_in == 2 * r + parity)
    return jnp.where(hit, 1.0, 0.0).astype(BF16)


def join_matrix(x):
    shape = (2 * x, 2 * x)
    row, col = iota(shape, 0), iota(shape, 1)
    half_in, x_in = col // x, col % x
    parity, half_out, r = row // x, (row % x) // (x // 2), row % (x // 2)
    hit = (half_in == half_out) & (x_in == 2 * r + parity)
    return jnp.where(hit, 1.0, 0.0).astype(BF16)


def weight_block(k_ref, a, b, xp):
    if a is None or b is None:
        return jnp.zeros((k_ref.shape[1], 2 * k_ref.shape[2]), BF16)
    at = (a * 3 + b) * 3
    if xp == 0:
        one = k_ref[at + 1]
        return jnp.concatenate([one, jnp.zeros_like(one)], axis=1)
    return jnp.concatenate([k_ref[at + 2], k_ref[at]], axis=1)


def forward_kernel(vol_ref, k_ref, v8_ref, send_ref, t_ref, x_ref, vs_ref, w_ref):
    cin, planes, ys, xs = vol_ref.shape
    cout = k_ref.shape[2]
    blocks = ys // 4
    quarter = 4 * cin
    for dp in range(2):
        cols = pl.ds(dp * 2 * cout, 2 * cout)
        for zp in range(2):
            for xp in range(2):
                for yp in range(2):
                    w_ref[pl.ds(((zp * 2 + yp) * 2 + xp) * cin, cin), cols] = weight_block(
                        k_ref, TAP[dp, zp], TAP[0, yp], xp
                    )
                w_ref[pl.ds(2 * quarter + (zp * 2 + xp) * cin, cin), cols] = weight_block(
                    k_ref, TAP[dp, zp], TAP[1, 1], xp
                )
    split = split_matrix(xs, False)
    split_swapped = split_matrix(xs, True)

    def prepare(z, carry):
        t_ref[...] = vol_ref[:, z].astype(F32).reshape(cin * ys, xs)
        for y in range(ys):
            k, h, yp = y // 4, (y // 2) % 2, y % 2
            rows = t_ref[pl.ds(y, cin, stride=ys), :]
            x_ref[yp, pl.ds(k * cin, cin), pl.ds(h * xs, xs)] = rows.astype(BF16)
        for yp in range(2):
            out = dot(x_ref[yp], split).astype(BF16)
            for k in range(blocks):
                for xp in range(2):
                    v8_ref[z, pl.ds((yp * 2 + xp) * cin, cin), pl.ds(k * xs, xs)] = out[
                        k * cin : (k + 1) * cin, xp * xs : (xp + 1) * xs
                    ]
        before = jnp.concatenate(
            [jnp.zeros((cin, xs), BF16), x_ref[1, : (blocks - 1) * cin, xs:]], axis=0
        )
        pair = jnp.concatenate([x_ref[1, :, :xs], before], axis=1)
        out = dot(pair, split_swapped).astype(BF16)
        for k in range(blocks):
            for xp in range(2):
                vs_ref[z, pl.ds(xp * cin, cin), pl.ds(k * xs, xs)] = out[
                    k * cin : (k + 1) * cin, xp * xs : (xp + 1) * xs
                ]
        return carry

    lax.fori_loop(0, planes, prepare, 0)
    weights = jnp.transpose(w_ref[...], (1, 0))
    group = 4
    width = group * xs
    first = iota((cout, width), 1) % (xs // 2) == 0

    def moved(value):
        return jnp.where(first, 0.0, pltpu.roll(value, 1, axis=1))

    def store(chunk, plane, value):
        value = value.astype(BF16)
        for kk in range(group):
            send_ref[chunk * group + kk, plane] = value[:, kk * xs : (kk + 1) * xs]

    def compute(chunk, carry):
        lanes = pl.ds(pl.multiple_of(chunk * width, width), width)
        left = None
        for p in range(planes // 2):
            rhs = jnp.concatenate(
                [
                    v8_ref[pl.ds(2 * p, 2), :, lanes].reshape(2 * quarter, width),
                    vs_ref[pl.ds(2 * p, 2), :, lanes].reshape(quarter, width),
                ],
                axis=0,
            )
            acc = dot(weights, rhs)
            here = acc[:cout] + moved(acc[cout : 2 * cout])
            after = acc[2 * cout : 3 * cout] + moved(acc[3 * cout :])
            store(chunk, p, here if left is None else here + left)
            left = after
        store(chunk, planes // 2, left)
        return carry

    lax.fori_loop(0, blocks // group, compute, 0)


def weight_kernel(recv_ref, v8_ref, gg_ref, part_ref):
    blocks, slots, cout, xs = recv_ref.shape
    planes, quarter, _ = v8_ref.shape
    cin = quarter // 4
    shape = (2 * xs, 3 * xs)
    row, col = iota(shape, 0), iota(shape, 1)
    variant, lane = col // xs + 1, col % xs
    dq, dr = variant // 2, variant % 2
    hit = (row == lane + dq * (xs // 2) + dr) & ((dr == 0) | (lane % (xs // 2) != xs // 2 - 1))
    shifts = jnp.where(hit, 1.0, 0.0).astype(BF16)

    def shifted(p, carry):
        here = recv_ref[:, p].reshape(blocks * cout, xs)
        after = jnp.concatenate([here[cout:], jnp.zeros((cout, xs), BF16)], axis=0)
        out = dot(jnp.concatenate([here, after], axis=1), shifts).astype(BF16)
        for k in range(blocks):
            lanes = pl.ds(k * xs, xs)
            rows = slice(k * cout, (k + 1) * cout)
            gg_ref[p, pl.ds(0, cout), lanes] = here[rows]
            for v in range(1, 4):
                gg_ref[p, pl.ds(v * cout, cout), lanes] = out[rows, (v - 1) * xs : v * xs]
        return carry

    lax.fori_loop(0, slots, shifted, 0)
    near, far = None, None
    for p in range(planes // 2):
        both = v8_ref[pl.ds(2 * p, 2)].reshape(2 * quarter, blocks * xs)
        one = dot_t(both, gg_ref[p])
        two = dot_t(v8_ref[2 * p + 1], gg_ref[p + 1])
        near = one if near is None else near + one
        far = two if far is None else far + two

    def piece(a, b, xp):
        dp, zp = [key for key, tap in TAP.items() if tap == a][0]
        dq, yp = [key for key, tap in TAP.items() if tap == b][0]
        at = (yp * 2 + xp) * cin
        if dp == 0:
            return near[zp * quarter + at : zp * quarter + at + cin, dq * 2 * cout : (dq + 1) * 2 * cout]
        return far[at : at + cin, dq * 2 * cout : (dq + 1) * 2 * cout]

    halves = []
    for a in range(3):
        for b in range(3):
            part_ref[pl.ds((a * 3 + b) * cin, cin), :] = piece(a, b, 1)
            halves.append(piece(a, b, 0)[:, :cout])
    halves.append(jnp.zeros((cin, cout), F32))
    for t in range(0, 10, 2):
        part_ref[pl.ds((9 + t // 2) * cin, cin), :] = jnp.concatenate(halves[t : t + 2], axis=1)
    rest = part_ref.shape[0] - 14 * cin
    if rest:
        part_ref[pl.ds(14 * cin, rest), :] = jnp.zeros((rest, 2 * cout), F32)


def input_kernel(gg_ref, k_ref, out_ref, w_ref, t_ref):
    cin, planes, ys, xs = out_ref.shape
    cout = k_ref.shape[2]
    blocks = ys // 4
    for zp in range(2):
        for yp in range(2):
            for xp in range(2):
                for dp in range(2):
                    for dq in range(2):
                        w_ref[
                            pl.ds(((zp * 2 + yp) * 2 + xp) * cin, cin),
                            pl.ds((dp * 2 + dq) * 2 * cout, 2 * cout),
                        ] = weight_block(k_ref, TAP[dp, zp], TAP[dq, yp], xp)
    join = join_matrix(xs)
    weights = w_ref[...]
    group = 4
    width = group * xs

    def one(p, carry):
        for chunk in range(blocks // group):
            lanes = pl.ds(chunk * width, width)
            rhs = gg_ref[pl.ds(p, 2), :, lanes].reshape(8 * cout, width)
            acc = dot(weights, rhs).astype(BF16)
            pairs = []
            for zy in range(4):
                even = acc[zy * 2 * cin : (zy * 2 + 1) * cin]
                odd = acc[(zy * 2 + 1) * cin : (zy * 2 + 2) * cin]
                for kk in range(group):
                    at = slice(kk * xs, (kk + 1) * xs)
                    pairs.append(jnp.concatenate([even[:, at], odd[:, at]], axis=1))
            joined = dot(jnp.concatenate(pairs, axis=0), join)
            for zy in range(4):
                for kk in range(group):
                    at = (zy * group + kk) * cin
                    for h in range(2):
                        y = 4 * (chunk * group + kk) + 2 * h + zy % 2
                        t_ref[zy // 2, pl.ds(y, cin, stride=ys), :] = joined[
                            at : at + cin, h * xs : (h + 1) * xs
                        ]
        for zp in range(2):
            out_ref[:, 2 * p + zp] = t_ref[zp].reshape(cin, ys, xs).astype(BF16)
        return carry

    lax.fori_loop(0, planes // 2, one, 0)


def final_kernel(sum_ref, out_ref, *, scale):
    _, cin, cout = out_ref.shape
    for t in range(9):
        full = sum_ref[pl.ds(t * cin, cin), :] * scale
        out_ref[3 * t + 2] = full[:, :cout]
        out_ref[3 * t] = full[:, cout:]
        half = sum_ref[pl.ds((9 + t // 2) * cin, cin), :] * scale
        out_ref[3 * t + 1] = half[:, (t % 2) * cout : (t % 2 + 1) * cout]


def call(kernel, outs, scratch=()):
    return pl.pallas_call(
        kernel,
        out_shape=outs,
        scratch_shapes=scratch,
        compiler_params=pltpu.CompilerParams(vmem_limit_bytes=48 << 20),
    )


def shards(volume, kernel, cotangent):
    count = lax.axis_size("gz")
    everyone = count * lax.axis_size("vol")
    _, cin, planes, ys, xs = volume.shape
    _, cout, ozs, band, oxs = cotangent.shape
    slots = planes // 2
    blocks = ys // 4
    lanes = blocks * xs
    taps = jnp.transpose(kernel, (2, 3, 4, 1, 0)).reshape(27, cin, cout)

    grads = jnp.transpose(cotangent[0], (1, 0, 2, 3)).reshape(count, slots, cout, band * oxs)
    above = jnp.concatenate([grads[1:, :1], jnp.zeros_like(grads[:1, :1])], axis=0)
    packed = jnp.concatenate([grads, above], axis=1)
    recv = lax.all_to_all(packed, "gz", 0, 0, tiled=True)
    if band != 2:
        recv = recv.reshape(blocks, 2, slots + 1, cout, oxs)
        recv = jnp.transpose(recv, (0, 2, 3, 1, 4)).reshape(blocks, slots + 1, cout, xs)

    v8, send = call(
        forward_kernel,
        (
            jax.ShapeDtypeStruct((planes, 4 * cin, lanes), BF16),
            jax.ShapeDtypeStruct((blocks, slots + 1, cout, xs), BF16),
        ),
        (
            pltpu.VMEM((cin * ys, xs), F32),
            pltpu.VMEM((2, blocks * cin, 2 * xs), BF16),
            pltpu.VMEM((planes, 2 * cin, lanes), BF16),
            pltpu.VMEM((12 * cin, 4 * cout), BF16),
        ),
    )(volume[0], taps)
    if band != 2:
        send = send.reshape(blocks, slots + 1, cout, 2, oxs)
        send = jnp.transpose(send, (0, 3, 1, 2, 4)).reshape(count, slots + 1, cout, band * oxs)
    back = lax.all_to_all(send, "gz", 0, 0, tiled=True)
    carried = jnp.concatenate([jnp.zeros_like(back[:1, slots:]), back[:-1, slots:]], axis=0)
    first = (back[:, :1].astype(F32) + carried.astype(F32)).astype(BF16)
    whole = jnp.concatenate([first, back[:, 1:slots]], axis=1)
    features = jnp.transpose(whole.reshape(ozs, cout, band, oxs), (1, 0, 2, 3))[None]

    rows = 14 * cin
    unit = 8 * everyone if rows >= 8 * everyone else everyone
    rows = -(-rows // unit) * unit
    gg, part = call(
        weight_kernel,
        (
            jax.ShapeDtypeStruct((slots + 1, 4 * cout, lanes), BF16),
            jax.ShapeDtypeStruct((rows, 2 * cout), F32),
        ),
    )(recv, v8)
    both = ("vol", "gz")
    spread = lax.all_to_all(part.reshape(everyone, rows // everyone, 2 * cout), both, 0, 0, tiled=True)
    total = jnp.sum(spread, axis=0)
    total = lax.all_to_all(jnp.broadcast_to(total, spread.shape), both, 0, 0, tiled=True)

    volume_grad = call(
        input_kernel,
        jax.ShapeDtypeStruct((cin, planes, ys, xs), BF16),
        (
            pltpu.VMEM((8 * cin, 8 * cout), BF16),
            pltpu.VMEM((2, cin * ys, xs), F32),
        ),
    )(gg, taps)[None]

    volumes = volume.shape[0] * lax.axis_size("vol")

    def finish(sum_ref, out_ref):
        final_kernel(sum_ref, out_ref, scale=1.0 / volumes)

    kernel_grad = call(finish, jax.ShapeDtypeStruct((27, cin, cout), F32))(
        total.reshape(rows, 2 * cout)
    )
    kernel_grad = jnp.transpose(kernel_grad.reshape(3, 3, 3, cin, cout), (4, 3, 0, 1, 2))
    return (features, volume_grad, kernel_grad)


def solution(mesh):
    placed = (P("vol", None, "gz", None, None), P(), P("vol", None, None, "gz", None))
    return jax.shard_map(
        shards,
        mesh=mesh,
        in_specs=placed,
        out_specs=(P("vol", None, None, "gz", None), P("vol", None, "gz", None, None), P()),
        check_vma=False,
    )
```

profile of v0, /device:TPU:0, one launch (start us, length us, event | category | flops | bytes accessed | tf_op | source)
XLA Modules:
  0.0 94.4 jit_solution(2436040286666374509)
XLA Ops:
  0.6 3.1 %reshape.30 = bf16[16,2,64,128]{3,1,0,2:T(2,128)(2,1)S(1)} reshape(bf16[32,64,2,64]{3,2,0,1:T(2,128)(2,1)} %bitcast.28) | data formatting | bytes 1048576 | tf_op jit(solution)/shard_map/reshape | solution.py:263
  3.7 0.2 copy.8
  4.0 0.0 copy-start.1
  4.0 0.0 copy-start.4
  4.0 1.0 %fusion.1 = bf16[16,3,64,128]{3,2,1,0:T(8,128)(2,1)} fusion(bf16[15,1,64,128]{3,2,1,0:T(8,128)(2,1)S(1)} %slice.19, bf16[16,2,64,128]{3,2,1,0:T(8,128)(2,1)S(1)} %copy.8), kind=kLoop, calls=%fused_computation.3 | loop fusion | flops 2359296 | bytes 1556480 | tf_op jit(solution)/shard_map/concatenate | solution.py:265
  4.9 7.4 %all-to-all-start.1 = ((bf16[16,3,64,128]{3,2,1,0:T(8,128)(2,1)}), bf16[16,3,64,128]{3,2,1,0:T(8,128)(2,1)S(1)}, u32[]{:S(2)}, u32[]{:S(2)}) async-start(bf16[16,3,64,128]{3,2,1,0:T(8,128)(2,1)} %fusion.1), calls=%async_computation.1 | async-start | bytes 1572864 | tf_op jit(solution)/shard_map/all_to_all | solution.py:266
  12.3 0.0 copy-done.1
  12.3 0.0 copy-done.4
  12.3 7.3 %shard_map.58 = (bf16[4,128,2048]{2,1,0:T(8,128)(2,1)S(1)}, bf16[16,3,64,128]{3,2,1,0:T(8,128)(2,1)}) custom-call(bf16[32,4,64,128]{3,2,1,0:T(8,128)(2,1)S(1)} %bitcast.22, bf16[27,32,64]{2,1,0:T(8,128)(2,1)S(1)} %bitcast.24), custom_call_target="tpu_custom_call" | custom-call | tf_op jit(solution)/shard_map/pallas_call | solution.py:271
  19.6 0.0 copy-start.2
  19.6 1.3 %copy-done.2 = bf16[4,128,2048]{2,1,0:T(8,128)(2,1)} copy-done((bf16[4,128,2048]{2,1,0:T(8,128)(2,1)}, bf16[4,128,2048]{2,1,0:T(8,128)(2,1)S(1)}, u32[]{:S(2)}) %copy-start.2) | copy-done | bytes 2097176
  21.0 10.1 %all-to-all-done.1.recv_ref = bf16[16,3,64,128]{3,2,1,0:T(8,128)(2,1)S(1)} async-done(((bf16[16,3,64,128]{3,2,1,0:T(8,128)(2,1)}), bf16[16,3,64,128]{3,2,1,0:T(8,128)(2,1)S(1)}, u32[]{:S(2)}, u32[]{:S(2)}) %all-to-all-start.1) | async-done | bytes 786464 | tf_op jit(solution)/shard_map/all_to_all | solution.py:266
  31.0 0.0 copy-start.3
  31.0 1.6 %copy-done.3 = bf16[4,128,2048]{2,1,0:T(8,128)(2,1)S(1)} copy-done((bf16[4,128,2048]{2,1,0:T(8,128)(2,1)S(1)}, bf16[4,128,2048]{2,1,0:T(8,128)(2,1)}, u32[]{:S(2)}) %copy-start.3) | copy-done | bytes 2097176
  32.6 4.1 %shard_map.59 = (bf16[3,256,2048]{2,1,0:T(8,128)(2,1)}, f32[512,128]{1,0:T(8,128)S(1)}) custom-call(bf16[16,3,64,128]{3,2,1,0:T(8,128)(2,1)S(1)} %all-to-all-done.1.recv_ref, bf16[4,128,2048]{2,1,0:T(8,128)(2,1)S(1)} %copy-done.3), custom_call_target="tpu_custom_call" | custom-call | tf_op jit(solution)/shard_map/pallas_call | solution.py:296
  36.7 15.4 %all_to_all.20 = f32[32,16,128]{2,1,0:T(8,128)S(1)} all-to-all(f32[32,16,128]{2,1,0:T(8,128)S(1)} %bitcast.26), channel_id=1, replica_groups=mesh['vol'=2,'gz'=16] {'vol','gz'}, dimensions={0} | all-to-all | bytes 524288 | tf_op jit(solution)/shard_map/all_to_all | solution.py:304
  52.1 3.6 %all-to-all-start = ((bf16[16,3,64,128]{3,2,1,0:T(8,128)(2,1)}), bf16[16,3,64,128]{3,2,1,0:T(8,128)(2,1)S(1)}, u32[]{:S(2)}, u32[]{:S(2)}) async-start(bf16[16,3,64,128]{3,2,1,0:T(8,128)(2,1)} %get-tuple-element.7), calls=%async_computation | async-start | bytes 1572864 | tf_op jit(solution)/shard_map/all_to_all | solution.py:287
  55.8 18.6 %all-to-all-done = bf16[16,3,64,128]{3,2,1,0:T(8,128)(2,1)S(1)} async-done(((bf16[16,3,64,128]{3,2,1,0:T(8,128)(2,1)}), bf16[16,3,64,128]{3,2,1,0:T(8,128)(2,1)S(1)}, u32[]{:S(2)}, u32[]{:S(2)}) %all-to-all-start) | async-done | bytes 786464 | tf_op jit(solution)/shard_map/all_to_all | solution.py:287
  74.4 0.7 broadcast_in_dim.11
  75.1 4.4 %all-to-all-start.3 = ((f32[32,16,128]{2,1,0:T(8,128)}), f32[32,16,128]{2,1,0:T(8,128)S(1)}, u32[]{:S(2)}, u32[]{:S(2)}) async-start(f32[32,16,128]{2,1,0:T(8,128)} %broadcast_in_dim.11), calls=%async_computation.3 | async-start | bytes 524288 | tf_op jit(solution)/shard_map/all_to_all | solution.py:306
  79.6 0.1 add_convert_fusion
  79.7 0.8 pad_maximum_fusion
  80.5 0.0 copy-start
  80.5 3.3 %reshape.25 = bf16[32,64,2,64]{3,2,1,0:T(2,128)(2,1)} reshape(bf16[16,2,64,128]{3,2,1,0:T(8,128)(2,1)} %pad_maximum_fusion) | data formatting | bytes 1048576 | tf_op jit(solution)/shard_map/reshape | solution.py:291
  83.8 0.0 copy-start.5
  83.8 3.4 %copy.10 = bf16[32,64,2,64]{3,2,0,1:T(2,128)(2,1)} copy(bf16[32,64,2,64]{3,2,1,0:T(2,128)(2,1)} %reshape.25) | data formatting | bytes 1048576 | tf_op jit(solution)/shard_map/reshape | solution.py:291
  87.2 0.0 copy-done
  87.2 0.0 copy-done.5
  87.2 6.3 %shard_map.60 = bf16[32,4,64,128]{3,2,1,0:T(8,128)(2,1)} custom-call(bf16[3,256,2048]{2,1,0:T(8,128)(2,1)S(1)} %copy-done, bf16[27,32,64]{2,1,0:T(8,128)(2,1)S(1)} %bitcast.25), custom_call_target="tpu_custom_call" | custom-call | tf_op jit(solution)/shard_map/pallas_call | solution.py:308
  93.5 0.0 all-to-all-done.3
  93.5 0.9 shard_map.61
  (4 shorter events, 0.1 us)
Async XLA Ops:
  4.0 8.4 %copy-start.1 = (bf16[1,32,4,64,128]{4,3,2,1,0:T(8,128)(2,1)S(1)}, bf16[1,32,4,64,128]{4,3,2,1,0:T(8,128)(2,1)}, u32[]{:S(2)}) copy-start(bf16[1,32,4,64,128]{4,3,2,1,0:T(8,128)(2,1)} %param.3) | copy-start | bytes 6291460
  4.0 8.4 %copy-start.4 = (bf16[64,32,3,3,3]{0,1,4,3,2:T(8,128)(2,1)S(1)}, bf16[64,32,3,3,3]{0,1,4,3,2:T(8,128)(2,1)}, u32[]{:S(2)}) copy-start(bf16[64,32,3,3,3]{0,1,4,3,2:T(8,128)(2,1)} %param.4) | copy-start | bytes 331780
  4.9 26.1 %all-to-all-start.1 = ((bf16[16,3,64,128]{3,2,1,0:T(8,128)(2,1)}), bf16[16,3,64,128]{3,2,1,0:T(8,128)(2,1)S(1)}, u32[]{:S(2)}, u32[]{:S(2)}) async-start(bf16[16,3,64,128]{3,2,1,0:T(8,128)(2,1)} %fusion.1), calls=%async_computation.1 | async-start | bytes 1572864 | tf_op jit(solution)/shard_map/all_to_all | solution.py:266
  19.6 1.3 %copy-start.2 = (bf16[4,128,2048]{2,1,0:T(8,128)(2,1)}, bf16[4,128,2048]{2,1,0:T(8,128)(2,1)S(1)}, u32[]{:S(2)}) copy-start(bf16[4,128,2048]{2,1,0:T(8,128)(2,1)S(1)} %get-tuple-element.8.v8_ref) | copy-start | bytes 6291460
  31.0 1.6 %copy-start.3 = (bf16[4,128,2048]{2,1,0:T(8,128)(2,1)S(1)}, bf16[4,128,2048]{2,1,0:T(8,128)(2,1)}, u32[]{:S(2)}) copy-start(bf16[4,128,2048]{2,1,0:T(8,128)(2,1)} %copy-done.2) | copy-start | bytes 6291460
  52.1 22.3 %all-to-all-start = ((bf16[16,3,64,128]{3,2,1,0:T(8,128)(2,1)}), bf16[16,3,64,128]{3,2,1,0:T(8,128)(2,1)S(1)}, u32[]{:S(2)}, u32[]{:S(2)}) async-start(bf16[16,3,64,128]{3,2,1,0:T(8,128)(2,1)} %get-tuple-element.7), calls=%async_computation | async-start | bytes 1572864 | tf_op jit(solution)/shard_map/all_to_all | solution.py:287
  75.1 18.4 %all-to-all-start.3 = ((f32[32,16,128]{2,1,0:T(8,128)}), f32[32,16,128]{2,1,0:T(8,128)S(1)}, u32[]{:S(2)}, u32[]{:S(2)}) async-start(f32[32,16,128]{2,1,0:T(8,128)} %broadcast_in_dim.11), calls=%async_computation.3 | async-start | bytes 524288 | tf_op jit(solution)/shard_map/all_to_all | solution.py:306
  80.5 6.7 %copy-start = (bf16[3,256,2048]{2,1,0:T(8,128)(2,1)S(1)}, bf16[3,256,2048]{2,1,0:T(8,128)(2,1)}, u32[]{:S(2)}) copy-start(bf16[3,256,2048]{2,1,0:T(8,128)(2,1)} %get-tuple-element.9.gg_ref) | copy-start | bytes 9437188
  83.8 3.4 %copy-start.5 = (bf16[64,32,3,3,3]{0,1,4,3,2:T(8,128)(2,1)S(1)}, bf16[64,32,3,3,3]{0,1,4,3,2:T(8,128)(2,1)}, u32[]{:S(2)}) copy-start(bf16[64,32,3,3,3]{0,1,4,3,2:T(8,128)(2,1)} %param.4) | copy-start | bytes 331780
where the time goes:
time: 94.9 us; the launch traced here: 94.4 us
  waiting for transfers between devices  28.6 us (30%)
  Pallas kernels  18.6 us (20%)
  starting transfers between devices  15.4 us (16%)
  blocking collectives  15.4 us (16%)
  local copies, waits for them, and re-layouts  13.7 us (14%)
  other arithmetic  1.91 us (2%)
    all_to_all x1, waiting for transfers between devices, shards(): back = lax.all_to_all(send, 'gz', 0, 0, tiled=True)  18.6 us
    all_to_all x1, blocking collectives, shards(): lax.all_to_all(part.reshape(everyone, rows // everyone, 2 * cout), both,...  15.4 us
    all_to_all x1, waiting for transfers between devices, shards(): recv = lax.all_to_all(packed, 'gz', 0, 0, tiled=True)  10.1 us
    all_to_all x1, starting transfers between devices, shards(): recv = lax.all_to_all(packed, 'gz', 0, 0, tiled=True)  7.39 us
    pallas_call x1, Pallas kernels, shards(): call(forward_kernel, (jax.ShapeDtypeStruct((planes, 4 * cin, lanes), BF16...  7.29 us
    reshape x2, local copies, waits for them, and re-layouts, shards(): whole.reshape(ozs, cout, band, oxs)  6.71 us
    pallas_call x1, Pallas kernels, shards(): call(input_kernel, jax.ShapeDtypeStruct((cin, planes, ys, xs), BF16), (pl...  6.31 us
    all_to_all x1, starting transfers between devices, shards(): lax.all_to_all(jnp.broadcast_to(total, spread.shape), both, 0, 0, tiled=T...  4.4 us
  transfers between devices with their start and end apart: 3, of which 2 were waited for; matrix products, arithmetic and copies ran while one was open for 8% of the time, Pallas kernels for 14%

commit v1 on v0

v1 whole, which is shorter than its diff:
```python
import jax
import jax.numpy as jnp
from jax import lax
from jax.experimental import pallas as pl
from jax.experimental.pallas import tpu as pltpu
from jax.sharding import PartitionSpec as P


F32 = jnp.float32
BF16 = jnp.bfloat16
TAP = {(0, 0): 1, (0, 1): 2, (1, 1): 0, (1, 0): None}


def dot(a, b):
    return lax.dot_general(a, b, (((1,), (0,)), ((), ())), preferred_element_type=F32)


def dot_t(a, b):
    return lax.dot_general(a, b, (((1,), (1,)), ((), ())), preferred_element_type=F32)


def iota(shape, dim):
    return lax.broadcasted_iota(jnp.int32, shape, dim)


def tap_matrix(x, swapped):
    shape = (2 * x, 3 * x)
    row, col = iota(shape, 0), iota(shape, 1)
    half_in, x_in = row // x, row % x
    tap, half_out, r = col // x, (col % x) // (x // 2), col % (x // 2)
    if swapped:
        half_out = 1 - half_out
    hit = (half_in == half_out) & (x_in == 2 * r + tap - 1)
    return jnp.where(hit, 1.0, 0.0).astype(BF16)


def join_matrix(x):
    shape = (2 * x, 2 * x)
    row, col = iota(shape, 0), iota(shape, 1)
    half_in, x_in = col // x, col % x
    parity, half_out, r = row // x, (row % x) // (x // 2), row % (x // 2)
    hit = (half_in == half_out) & (x_in == 2 * r + parity)
    return jnp.where(hit, 1.0, 0.0).astype(BF16)


def shift_matrix(x):
    shape = (2 * x, 3 * x)
    row, col = iota(shape, 0), iota(shape, 1)
    variant, lane = col // x + 1, col % x
    dq, dr = variant // 2, variant % 2
    hit = (row == lane + dq * (x // 2) + dr) & ((dr == 0) | (lane % (x // 2) != x // 2 - 1))
    return jnp.where(hit, 1.0, 0.0).astype(BF16)


def weight_block(k_ref, a, b, xp):
    if a is None or b is None:
        return jnp.zeros((k_ref.shape[1], 2 * k_ref.shape[2]), BF16)
    at = (a * 3 + b) * 3
    if xp == 0:
        one = k_ref[at + 1]
        return jnp.concatenate([one, jnp.zeros_like(one)], axis=1)
    return jnp.concatenate([k_ref[at + 2], k_ref[at]], axis=1)


def forward_kernel(vol_ref, k_ref, xx_ref, send_ref, t_ref, x_ref):
    cin, planes, ys, xs = vol_ref.shape
    cout = k_ref.shape[2]
    blocks = ys // 4
    split = tap_matrix(xs, False)
    split_swapped = tap_matrix(xs, True)

    def prepare(z, carry):
        t_ref[...] = vol_ref[:, z].astype(F32).reshape(cin * ys, xs)
        for y in range(ys):
            k, h, yp = y // 4, (y // 2) % 2, y % 2
            rows = t_ref[pl.ds(y, cin, stride=ys), :]
            x_ref[yp, pl.ds(k * cin, cin), pl.ds(h * xs, xs)] = rows.astype(BF16)
        before = jnp.concatenate(
            [jnp.zeros((cin, xs), BF16), x_ref[1, : (blocks - 1) * cin, xs:]], axis=0
        )
        swapped = jnp.concatenate([x_ref[1, :, :xs], before], axis=1)
        for b, (pair, matrix) in enumerate(
            [(swapped, split_swapped), (x_ref[0], split), (x_ref[1], split)]
        ):
            out = dot(pair, matrix).astype(BF16)
            for k in range(blocks):
                for e in range(3):
                    xx_ref[z, pl.ds((b * 3 + e) * cin, cin), pl.ds(k * xs, xs)] = out[
                        k * cin : (k + 1) * cin, e * xs : (e + 1) * xs
                    ]
        return carry

    lax.fori_loop(0, planes, prepare, 0)
    w = k_ref[...].reshape(3, 9 * cin, cout)
    even = jnp.transpose(w[1], (1, 0))
    odd = jnp.transpose(jnp.concatenate([w[2], w[0]], axis=1), (1, 0))
    group = 4
    width = group * xs

    def store(chunk, plane, value):
        value = value.astype(BF16)
        for kk in range(group):
            send_ref[chunk * group + kk, plane] = value[:, kk * xs : (kk + 1) * xs]

    def compute(chunk, carry):
        lanes = pl.ds(pl.multiple_of(chunk * width, width), width)
        left = None
        for p in range(planes // 2):
            low = dot(even, xx_ref[2 * p, :, lanes])
            high = dot(odd, xx_ref[2 * p + 1, :, lanes])
            here = low + high[:cout]
            store(chunk, p, here if left is None else here + left)
            left = high[cout:]
        store(chunk, planes // 2, left)
        return carry

    lax.fori_loop(0, blocks // group, compute, 0)


def weight_kernel(recv_ref, xx_ref, send_ref, mix_ref):
    blocks, slots, _, xs = recv_ref.shape
    planes, rows, _ = xx_ref.shape
    count, feature_rows, _ = send_ref.shape
    unit = mix_ref.shape[1] - feature_rows
    for k in range(count):
        mix_ref[k, pl.ds(0, feature_rows), :] = send_ref[k]
    grads = [
        jnp.concatenate([recv_ref[k, p] for k in range(blocks)], axis=1) for p in range(slots)
    ]
    low, high = None, None
    for p in range(planes // 2):
        one = dot_t(xx_ref[2 * p], grads[p])
        two = dot_t(xx_ref[2 * p + 1], jnp.concatenate([grads[p], grads[p + 1]], axis=0))
        low = one if low is None else low + one
        high = two if high is None else high + two
    part = jnp.concatenate(
        [
            high,
            jnp.concatenate([low[: rows // 2], low[rows // 2 :]], axis=1),
            jnp.zeros((count * unit - rows - rows // 2, xs), F32),
        ],
        axis=0,
    ).astype(BF16)
    for k in range(count):
        mix_ref[k, pl.ds(feature_rows, unit), :] = part[k * unit : (k + 1) * unit]


def sum_kernel(back_ref, total_ref, *, scale):
    count, rows, _ = back_ref.shape
    everyone, unit, _ = total_ref.shape
    total = None
    for k in range(count):
        piece = back_ref[k, pl.ds(rows - unit, unit), :].astype(F32)
        total = piece if total is None else total + piece
    total = (total * scale).astype(BF16)
    for k in range(everyone):
        total_ref[k] = total


def final_kernel(total_ref, out_ref):
    _, rows, cout = out_ref.shape
    volumes, count, unit, xs = total_ref.shape
    total = total_ref[0].astype(F32)
    for v in range(1, volumes):
        total = total + total_ref[v].astype(F32)
    total = total.reshape(count * unit, xs)
    high = total[:rows]
    low = total[rows : rows + rows // 2]
    out_ref[2] = high[:, :cout]
    out_ref[0] = high[:, cout:]
    out_ref[1] = jnp.concatenate([low[:, :cout], low[:, cout:]], axis=0)


def input_kernel(recv_ref, k_ref, out_ref, gg_ref, w_ref, t_ref):
    cin, planes, ys, xs = out_ref.shape
    blocks, slots, cout, _ = recv_ref.shape
    shifts = shift_matrix(xs)

    def shifted(p, carry):
        here = recv_ref[:, p].reshape(blocks * cout, xs)
        after = jnp.concatenate([here[cout:], jnp.zeros((cout, xs), BF16)], axis=0)
        out = dot(jnp.concatenate([here, after], axis=1), shifts).astype(BF16)
        for k in range(blocks):
            lanes = pl.ds(k * xs, xs)
            rows = slice(k * cout, (k + 1) * cout)
            gg_ref[p, pl.ds(0, cout), lanes] = here[rows]
            for v in range(1, 4):
                gg_ref[p, pl.ds(v * cout, cout), lanes] = out[rows, (v - 1) * xs : v * xs]
        return carry

    lax.fori_loop(0, slots, shifted, 0)
    for zp in range(2):
        for yp in range(2):
            for xp in range(2):
                for dp in range(2):
                    for dq in range(2):
                        w_ref[
                            pl.ds(((zp * 2 + yp) * 2 + xp) * cin, cin),
                            pl.ds((dp * 2 + dq) * 2 * cout, 2 * cout),
                        ] = weight_block(k_ref, TAP[dp, zp], TAP[dq, yp], xp)
    join = join_matrix(xs)
    weights = w_ref[...]
    group = 4
    width = group * xs

    def one(p, carry):
        for chunk in range(blocks // group):
            lanes = pl.ds(chunk * width, width)
            rhs = gg_ref[pl.ds(p, 2), :, lanes].reshape(8 * cout, width)
            acc = dot(weights, rhs).astype(BF16)
            pairs = []
            for zy in range(4):
                even = acc[zy * 2 * cin : (zy * 2 + 1) * cin]
                odd = acc[(zy * 2 + 1) * cin : (zy * 2 + 2) * cin]
                for kk in range(group):
                    at = slice(kk * xs, (kk + 1) * xs)
                    pairs.append(jnp.concatenate([even[:, at], odd[:, at]], axis=1))
            joined = dot(jnp.concatenate(pairs, axis=0), join)
            for zy in range(4):
                for kk in range(group):
                    at = (zy * group + kk) * cin
                    for h in range(2):
                        y = 4 * (chunk * group + kk) + 2 * h + zy % 2
                        t_ref[zy // 2, pl.ds(y, cin, stride=ys), :] = joined[
                            at : at + cin, h * xs : (h + 1) * xs
                        ]
        for zp in range(2):
            out_ref[:, 2 * p + zp] = t_ref[zp].reshape(cin, ys, xs).astype(BF16)
        return carry

    lax.fori_loop(0, planes // 2, one, 0)


def call(kernel, outs, scratch=(), mib=24):
    return pl.pallas_call(
        kernel,
        out_shape=outs,
        scratch_shapes=scratch,
        compiler_params=pltpu.CompilerParams(vmem_limit_bytes=mib << 20),
    )


def shards(volume, kernel, cotangent):
    count = lax.axis_size("gz")
    everyone = count * lax.axis_size("vol")
    _, cin, planes, ys, xs = volume.shape
    _, cout, ozs, band, oxs = cotangent.shape
    slots = planes // 2
    blocks = ys // 4
    lanes = blocks * xs
    taps = jnp.transpose(kernel, (2, 3, 4, 1, 0)).reshape(27, cin, cout)

    grads = jnp.transpose(cotangent[0], (1, 0, 2, 3)).reshape(count, slots, cout, band * oxs)
    above = jnp.concatenate([grads[1:, :1], jnp.zeros_like(grads[:1, :1])], axis=0)
    packed = jnp.concatenate([grads, above], axis=1)
    recv = lax.all_to_all(packed, "gz", 0, 0, tiled=True)
    if band != 2:
        recv = recv.reshape(blocks, 2, slots + 1, cout, oxs)
        recv = jnp.transpose(recv, (0, 2, 3, 1, 4)).reshape(blocks, slots + 1, cout, xs)

    xx, send = call(
        forward_kernel,
        (
            jax.ShapeDtypeStruct((planes, 9 * cin, lanes), BF16),
            jax.ShapeDtypeStruct((blocks, slots + 1, cout, xs), BF16),
        ),
        (pltpu.VMEM((cin * ys, xs), F32), pltpu.VMEM((2, blocks * cin, 2 * xs), BF16)),
    )(volume[0], taps)
    if band != 2:
        send = send.reshape(blocks, slots + 1, cout, 2, oxs)
        send = jnp.transpose(send, (0, 3, 1, 2, 4)).reshape(count, slots + 1, cout, band * oxs)
        send = jnp.pad(send, ((0, 0), (0, 0), (0, 0), (0, xs - band * oxs)))
    send = send.reshape(count, (slots + 1) * cout, xs)
    unit = -(-(27 * cin // 2) // (16 * count)) * 16
    mix = call(
        weight_kernel,
        jax.ShapeDtypeStruct((count, (slots + 1) * cout + unit, xs), BF16),
    )(recv, xx, send)
    back = lax.all_to_all(mix, "gz", 0, 0, tiled=True)
    volumes = volume.shape[0] * lax.axis_size("vol")

    def add(back_ref, total_ref):
        sum_kernel(back_ref, total_ref, scale=1.0 / volumes)

    total = call(add, jax.ShapeDtypeStruct((everyone, unit, xs), BF16))(back)
    total = lax.all_to_all(total, ("vol", "gz"), 0, 0, tiled=True)
    back = back[:, : (slots + 1) * cout].reshape(count, slots + 1, cout, xs)
    carried = jnp.concatenate([jnp.zeros_like(back[:1, slots:]), back[:-1, slots:]], axis=0)
    first = (back[:, :1].astype(F32) + carried.astype(F32)).astype(BF16)
    whole = jnp.concatenate([first, back[:, 1:slots]], axis=1)
    whole = whole[..., : band * oxs].reshape(ozs, cout, band, oxs)
    features = jnp.transpose(whole, (1, 0, 2, 3))[None]

    volume_grad = call(
        input_kernel,
        jax.ShapeDtypeStruct((cin, planes, ys, xs), BF16),
        (
            pltpu.VMEM((slots + 1, 4 * cout, lanes), BF16),
            pltpu.VMEM((8 * cin, 8 * cout), BF16),
            pltpu.VMEM((2, cin * ys, xs), F32),
        ),
    )(recv, taps)[None]

    kernel_grad = call(final_kernel, jax.ShapeDtypeStruct((3, 9 * cin, cout), F32))(
        total.reshape(everyone // count, count, unit, xs)
    )
    kernel_grad = jnp.transpose(kernel_grad.reshape(3, 3, 3, cin, cout), (4, 3, 0, 1, 2))
    return (features, volume_grad, kernel_grad)


def solution(mesh):
    placed = (P("vol", None, "gz", None, None), P(), P("vol", None, None, "gz", None))
    return jax.shard_map(
        shards,
        mesh=mesh,
        in_specs=placed,
        out_specs=(P("vol", None, None, "gz", None), P("vol", None, "gz", None, None), P()),
        check_vma=False,
    )
```

time: 94.9 us -> 79.1 us (0.83)
  waiting for transfers between devices: 28.6 us -> 8.81 us
  blocking collectives: 15.4 us -> 27.6 us
  starting transfers between devices: 15.4 us -> 11.8 us
  local copies, waits for them, and re-layouts: 13.7 us -> 11.4 us
  Pallas kernels: 18.6 us -> 17.2 us
    all_to_all x2 -> x1, waiting for transfers between devices: 18.6 us -> 0.36 us  [shards(): total = lax.all_to_all(total, ('vol', 'gz'), 0, 0, tiled=True)]
    all_to_all x1, blocking collectives: 15.4 us -> 27.6 us  [shards(): back = lax.all_to_all(mix, 'gz', 0, 0, tiled=True)]
    reshape x2 -> x1, local copies, waits for them, and re-layouts: 6.71 us -> 1.39 us  [shards(): whole = whole[..., :band * oxs].reshape(ozs, cout, band, oxs)]
    all_to_all x2 -> x1, starting transfers between devices: 8.01 us -> 4.43 us  [shards(): total = lax.all_to_all(total, ('vol', 'gz'), 0, 0, tiled=True)]
    unnamed x12 -> x8, local copies, waits for them, and re-layouts: 2.93 us -> 6.06 us
    pallas_call x3 -> x4, Pallas kernels: 12.3 us -> 9.53 us  [the longest x1 6.48 us: shards(): call(forward_kernel, (jax.ShapeDtypeStruct((planes, 9 * cin, lanes), BF16...]
    all_to_all x1, waiting for transfers between devices: 10.1 us -> 8.44 us  [shards(): recv = lax.all_to_all(packed, 'gz', 0, 0, tiled=True)]
    pallas_call x1, Pallas kernels: 6.31 us -> 7.7 us  [shards(): call(input_kernel, jax.ShapeDtypeStruct((cin, planes, ys, xs), BF16), (pl...]
  transfers between devices with their start and end apart: 3 -> 2, of which waited for: 2 -> 2; matrix products, arithmetic and copies ran while one was open for 8% -> 3% of each run, Pallas kernels for 14% -> 18%
where the time goes in v1:
time: 79.1 us; the launch traced here: 78.7 us
  blocking collectives  27.6 us (35%)
  Pallas kernels  17.2 us (22%)
  starting transfers between devices  11.8 us (15%)
  local copies, waits for them, and re-layouts  11.4 us (14%)
  waiting for transfers between devices  8.81 us (11%)
  other arithmetic  1.08 us (1%)
    all_to_all x1, blocking collectives, shards(): back = lax.all_to_all(mix, 'gz', 0, 0, tiled=True)  27.6 us
    all_to_all x1, waiting for transfers between devices, shards(): recv = lax.all_to_all(packed, 'gz', 0, 0, tiled=True)  8.44 us
    pallas_call x1, Pallas kernels, shards(): call(input_kernel, jax.ShapeDtypeStruct((cin, planes, ys, xs), BF16), (pl...  7.7 us
    all_to_all x1, starting transfers between devices, shards(): recv = lax.all_to_all(packed, 'gz', 0, 0, tiled=True)  7.39 us
    pallas_call x1, Pallas kernels, shards(): call(forward_kernel, (jax.ShapeDtypeStruct((planes, 9 * cin, lanes), BF16...  6.48 us
    unnamed x8, local copies, waits for them, and re-layouts  6.06 us
    all_to_all x1, starting transfers between devices, shards(): total = lax.all_to_all(total, ('vol', 'gz'), 0, 0, tiled=True)  4.43 us
    reshape x2, local copies, waits for them, and re-layouts, shards(): jnp.transpose(cotangent[0], (1, 0, 2, 3))  3.28 us
  transfers between devices with their start and end apart: 2, of which 2 were waited for; matrix products, arithmetic and copies ran while one was open for 3% of the time, Pallas kernels for 18%

profile of v1, /device:TPU:0, one launch (start us, length us, event | category | flops | bytes accessed | tf_op | source)
XLA Modules:
  0.0 78.7 jit_solution(6754788234338173033)
XLA Ops:
  0.6 3.1 %reshape.34 = bf16[16,2,64,128]{3,1,0,2:T(2,128)(2,1)S(1)} reshape(bf16[32,64,2,64]{3,2,0,1:T(2,128)(2,1)} %bitcast.30) | data formatting | bytes 1048576 | tf_op jit(solution)/shard_map/reshape | solution.py:253
  3.7 0.2 copy.8
  4.0 0.0 copy-start.3
  4.0 1.0 %fusion.1 = bf16[16,3,64,128]{3,2,1,0:T(8,128)(2,1)} fusion(bf16[15,1,64,128]{3,2,1,0:T(8,128)(2,1)S(1)} %slice.20, bf16[16,2,64,128]{3,2,1,0:T(8,128)(2,1)S(1)} %copy.8), kind=kLoop, calls=%fused_computation.2 | loop fusion | flops 2359296 | bytes 1556480 | tf_op jit(solution)/shard_map/concatenate | solution.py:255
  4.9 7.4 %all-to-all-start = ((bf16[16,3,64,128]{3,2,1,0:T(8,128)(2,1)}), bf16[16,3,64,128]{3,2,1,0:T(8,128)(2,1)S(1)}, u32[]{:S(2)}, u32[]{:S(2)}) async-start(bf16[16,3,64,128]{3,2,1,0:T(8,128)(2,1)} %fusion.1), calls=%async_computation | async-start | bytes 1572864 | tf_op jit(solution)/shard_map/all_to_all | solution.py:256
  12.3 0.0 copy-done.3
  12.3 0.0 copy-start.2
  12.3 1.6 %copy-done.2 = bf16[1,32,4,64,128]{4,3,2,1,0:T(8,128)(2,1)S(1)} copy-done((bf16[1,32,4,64,128]{4,3,2,1,0:T(8,128)(2,1)S(1)}, bf16[1,32,4,64,128]{4,3,2,1,0:T(8,128)(2,1)}, u32[]{:S(2)}) %copy-start.2) | copy-done | bytes 2097176
  13.9 6.5 %shard_map.58 = (bf16[4,288,2048]{2,1,0:T(8,128)(2,1)S(1)}, bf16[16,3,64,128]{3,2,1,0:T(8,128)(2,1)S(1)}) custom-call(bf16[32,4,64,128]{3,2,1,0:T(8,128)(2,1)S(1)} %bitcast.21, bf16[27,32,64]{2,1,0:T(8,128)(2,1)S(1)} %bitcast.23), custom_call_target="tpu_custom_call" | custom-call | tf_op jit(solution)/shard_map/pallas_call | solution.py:261
  20.4 0.0 copy-start
  20.4 2.1 %copy-done = bf16[4,288,2048]{2,1,0:T(8,128)(2,1)} copy-done((bf16[4,288,2048]{2,1,0:T(8,128)(2,1)}, bf16[4,288,2048]{2,1,0:T(8,128)(2,1)S(1)}, u32[]{:S(2)}) %copy-start) | copy-done | bytes 4718616
  22.5 8.4 %all-to-all-done.recv_ref = bf16[16,3,64,128]{3,2,1,0:T(8,128)(2,1)S(1)} async-done(((bf16[16,3,64,128]{3,2,1,0:T(8,128)(2,1)}), bf16[16,3,64,128]{3,2,1,0:T(8,128)(2,1)S(1)}, u32[]{:S(2)}, u32[]{:S(2)}) %all-to-all-start) | async-done | bytes 786464 | tf_op jit(solution)/shard_map/all_to_all | solution.py:256
  31.0 0.0 copy-start.1
  31.0 2.3 %copy-done.1 = bf16[4,288,2048]{2,1,0:T(8,128)(2,1)S(1)} copy-done((bf16[4,288,2048]{2,1,0:T(8,128)(2,1)S(1)}, bf16[4,288,2048]{2,1,0:T(8,128)(2,1)}, u32[]{:S(2)}) %copy-start.1) | copy-done | bytes 4718616
  33.3 1.4 %shard_map.59 = bf16[16,224,128]{2,1,0:T(8,128)(2,1)S(1)} custom-call(bf16[16,3,64,128]{3,2,1,0:T(8,128)(2,1)S(1)} %all-to-all-done.recv_ref, bf16[4,288,2048]{2,1,0:T(8,128)(2,1)S(1)} %copy-done.1, bf16[16,192,128]{2,1,0:T(8,128)(2,1)S(1)} %bitcast.25), custom_call_target="tpu_custom_call" | custom-call | tf_op jit(solution)/shard_map/pallas_call | solution.py:275
  34.8 27.6 %all_to_all.15.back_ref = bf16[16,224,128]{2,1,0:T(8,128)(2,1)S(1)} all-to-all(bf16[16,224,128]{2,1,0:T(8,128)(2,1)S(1)} %shard_map.59), channel_id=1, replica_groups=mesh['vol'=2,'gz'=16] {'gz'}, dimensions={0} | all-to-all | bytes 1835008 | tf_op jit(solution)/shard_map/all_to_all | solution.py:279
  62.3 0.7 shard_map.61
  63.1 4.4 %all-to-all-start.2 = ((bf16[32,32,128]{2,1,0:T(8,128)(2,1)}), bf16[32,32,128]{2,1,0:T(8,128)(2,1)S(1)}, u32[]{:S(2)}, u32[]{:S(2)}) async-start(bf16[32,32,128]{2,1,0:T(8,128)(2,1)} %shard_map.61), calls=%async_computation.2 | async-start | bytes 524288 | tf_op jit(solution)/shard_map/all_to_all | solution.py:286
  67.5 7.7 %shard_map.60 = bf16[32,4,64,128]{3,2,1,0:T(8,128)(2,1)} custom-call(bf16[16,3,64,128]{3,2,1,0:T(8,128)(2,1)S(1)} %all-to-all-done.recv_ref, bf16[27,32,64]{2,1,0:T(8,128)(2,1)S(1)} %bitcast.24), custom_call_target="tpu_custom_call" | custom-call | tf_op jit(solution)/shard_map/pallas_call | solution.py:294
  75.2 0.1 slice.21
  75.3 0.1 add_convert_fusion
  75.4 0.1 pad_maximum_fusion
  75.5 0.5 copy.7
  76.0 1.4 %reshape.31 = bf16[32,64,2,64]{3,2,0,1:T(2,128)(2,1)} reshape(bf16[16,2,64,128]{3,1,0,2:T(2,128)(2,1)S(1)} %copy.7) | data formatting | bytes 1048576 | tf_op jit(solution)/shard_map/reshape | solution.py:291
  77.4 0.4 all-to-all-done.2
  77.8 0.9 %shard_map.62 = f32[3,288,64]{2,1,0:T(8,128)} custom-call(bf16[2,16,32,128]{3,2,1,0:T(8,128)(2,1)S(1)} %bitcast.22), custom_call_target="tpu_custom_call" | custom-call | tf_op jit(solution)/shard_map/pallas_call | solution.py:304
  (3 shorter events, 0.1 us)
Async XLA Ops:
  4.0 8.4 %copy-start.3 = (bf16[64,32,3,3,3]{0,1,4,3,2:T(8,128)(2,1)S(1)}, bf16[64,32,3,3,3]{0,1,4,3,2:T(8,128)(2,1)}, u32[]{:S(2)}) copy-start(bf16[64,32,3,3,3]{0,1,4,3,2:T(8,128)(2,1)} %param.4) | copy-start | bytes 331780
  4.9 26.1 %all-to-all-start = ((bf16[16,3,64,128]{3,2,1,0:T(8,128)(2,1)}), bf16[16,3,64,128]{3,2,1,0:T(8,128)(2,1)S(1)}, u32[]{:S(2)}, u32[]{:S(2)}) async-start(bf16[16,3,64,128]{3,2,1,0:T(8,128)(2,1)} %fusion.1), calls=%async_computation | async-start | bytes 1572864 | tf_op jit(solution)/shard_map/all_to_all | solution.py:256
  12.3 1.6 %copy-start.2 = (bf16[1,32,4,64,128]{4,3,2,1,0:T(8,128)(2,1)S(1)}, bf16[1,32,4,64,128]{4,3,2,1,0:T(8,128)(2,1)}, u32[]{:S(2)}) copy-start(bf16[1,32,4,64,128]{4,3,2,1,0:T(8,128)(2,1)} %param.3) | copy-start | bytes 6291460
  20.4 2.1 %copy-start = (bf16[4,288,2048]{2,1,0:T(8,128)(2,1)}, bf16[4,288,2048]{2,1,0:T(8,128)(2,1)S(1)}, u32[]{:S(2)}) copy-start(bf16[4,288,2048]{2,1,0:T(8,128)(2,1)S(1)} %get-tuple-element.5.xx_ref) | copy-start | bytes 14155780
  31.0 2.3 %copy-start.1 = (bf16[4,288,2048]{2,1,0:T(8,128)(2,1)S(1)}, bf16[4,288,2048]{2,1,0:T(8,128)(2,1)}, u32[]{:S(2)}) copy-start(bf16[4,288,2048]{2,1,0:T(8,128)(2,1)} %copy-done) | copy-start | bytes 14155780
  63.1 14.7 %all-to-all-start.2 = ((bf16[32,32,128]{2,1,0:T(8,128)(2,1)}), bf16[32,32,128]{2,1,0:T(8,128)(2,1)S(1)}, u32[]{:S(2)}, u32[]{:S(2)}) async-start(bf16[32,32,128]{2,1,0:T(8,128)(2,1)} %shard_map.61), calls=%async_computation.2 | async-start | bytes 524288 | tf_op jit(solution)/shard_map/all_to_all | solution.py:286

commit v2 on v1

--- a/solution.py
+++ b/solution.py
@@ -62,15 +62,42 @@
     return jnp.concatenate([k_ref[at + 2], k_ref[at]], axis=1)
 
 
-def forward_kernel(vol_ref, k_ref, xx_ref, send_ref, t_ref, x_ref):
+def pack_kernel(cot_ref, vol_ref, packed_ref, plane_ref, c_ref, s_ref, sems):
+    parts = c_ref.shape[0]
+    copy = pltpu.make_async_copy(vol_ref.at[:, vol_ref.shape[1] - 1], plane_ref, sems.at[parts])
+    copy.start()
+    size = cot_ref.shape[0] // parts
+    loads = [
+        pltpu.make_async_copy(cot_ref.at[pl.ds(i * size, size)], c_ref.at[i], sems.at[i])
+        for i in range(parts)
+    ]
+    for load in loads:
+        load.start()
+    count, slots, cout, xs = packed_ref.shape
+    half = cot_ref.shape[1]
+    own = cout // parts
+    stride = size // own
+    left = iota((own, xs), 1) < half
+    for i in range(parts):
+        loads[i].wait()
+        s_ref[:, :half] = c_ref[i].astype(F32)
+        for p in range(count * slots):
+            low = s_ref[pl.ds(2 * p, own, stride=stride), :]
+            high = s_ref[pl.ds(2 * p + 1, own, stride=stride), :]
+            both = jnp.where(left, low, pltpu.roll(high, half, axis=1))
+            packed_ref[p // slots, p % slots, pl.ds(i * own, own)] = both.astype(BF16)
+    copy.wait()
+
+
+def forward_kernel(vol_ref, halo_ref, k_ref, out_ref, mix_ref, xx_ref, t_ref, x_ref, sems):
     cin, planes, ys, xs = vol_ref.shape
     cout = k_ref.shape[2]
     blocks = ys // 4
     split = tap_matrix(xs, False)
     split_swapped = tap_matrix(xs, True)
 
-    def prepare(z, carry):
-        t_ref[...] = vol_ref[:, z].astype(F32).reshape(cin * ys, xs)
+    def expand(plane, z):
+        t_ref[...] = plane.astype(F32).reshape(cin * ys, xs)
         for y in range(ys):
             k, h, yp = y // 4, (y // 2) % 2, y % 2
             rows = t_ref[pl.ds(y, cin, stride=ys), :]
@@ -88,61 +115,97 @@
                     xx_ref[z, pl.ds((b * 3 + e) * cin, cin), pl.ds(k * xs, xs)] = out[
                         k * cin : (k + 1) * cin, e * xs : (e + 1) * xs
                     ]
+
+    def leave(z):
+        return pltpu.make_async_copy(
+            xx_ref.at[z, pl.ds(3 * cin, 6 * cin)], out_ref.at[z], sems.at[z]
+        )
+
+    def own(z, carry):
+        expand(vol_ref[:, z], z + 1)
+        leave(z + 1).start()
         return carry
 
-    lax.fori_loop(0, planes, prepare, 0)
-    w = k_ref[...].reshape(3, 9 * cin, cout)
-    even = jnp.transpose(w[1], (1, 0))
-    odd = jnp.transpose(jnp.concatenate([w[2], w[0]], axis=1), (1, 0))
+    lax.fori_loop(0, planes, own, 0)
+    expand(halo_ref[...], 0)
+    leave(0).start()
+    weights = jnp.transpose(k_ref[...].reshape(27 * cin, cout), (1, 0))
     group = 4
     width = group * xs
 
-    def store(chunk, plane, value):
-        value = value.astype(BF16)
-        for kk in range(group):
-            send_ref[chunk * group + kk, plane] = value[:, kk * xs : (kk + 1) * xs]
-
     def compute(chunk, carry):
         lanes = pl.ds(pl.multiple_of(chunk * width, width), width)
-        left = None
         for p in range(planes // 2):
-            low = dot(even, xx_ref[2 * p, :, lanes])
-            high = dot(odd, xx_ref[2 * p + 1, :, lanes])
-            here = low + high[:cout]
-            store(chunk, p, here if left is None else here + left)
-            left = high[cout:]
-        store(chunk, planes // 2, left)
+            rhs = xx_ref[2 * p : 2 * p + 3, :, lanes].reshape(27 * cin, width)
+            value = dot(weights, rhs).astype(BF16)
+            for kk in range(group):
+                mix_ref[chunk * group + kk, pl.ds(p * cout, cout), :] = value[
+                    :, kk * xs : (kk + 1) * xs
+                ]
         return carry
 
     lax.fori_loop(0, blocks // group, compute, 0)
-
-
-def weight_kernel(recv_ref, xx_ref, send_ref, mix_ref):
-    blocks, slots, _, xs = recv_ref.shape
+    unit = mix_ref.shape[1] - planes // 2 * cout
+    mix_ref[:, pl.ds(planes // 2 * cout, unit), :] = jnp.zeros((blocks, unit, xs), BF16)
+    for z in range(planes + 1):
+        leave(z).wait()
+
+
+def weight_kernel(recv_ref, xx_ref, mix_in_ref, mix_ref, xx_vmem, part_vmem, sems):
+    del mix_in_ref
+    blocks, slots, cout, xs = recv_ref.shape
     planes, rows, _ = xx_ref.shape
-    count, feature_rows, _ = send_ref.shape
-    unit = mix_ref.shape[1] - feature_rows
-    for k in range(count):
-        mix_ref[k, pl.ds(0, feature_rows), :] = send_ref[k]
+    count, unit, _ = part_vmem.shape
+    copies = [
+        pltpu.make_async_copy(xx_ref.at[z], xx_vmem.at[z], sems.at[z]) for z in range(planes)
+    ]
+    third = rows // 2
+    for z in range(0, planes, 2):
+        copies[z].start()
     grads = [
         jnp.concatenate([recv_ref[k, p] for k in range(blocks)], axis=1) for p in range(slots)
     ]
-    low, high = None, None
-    for p in range(planes // 2):
-        one = dot_t(xx_ref[2 * p], grads[p])
-        two = dot_t(xx_ref[2 * p + 1], jnp.concatenate([grads[p], grads[p + 1]], axis=0))
-        low = one if low is None else low + one
-        high = two if high is None else high + two
-    part = jnp.concatenate(
-        [
-            high,
-            jnp.concatenate([low[: rows // 2], low[rows // 2 :]], axis=1),
-            jnp.zeros((count * unit - rows - rows // 2, xs), F32),
-        ],
-        axis=0,
-    ).astype(BF16)
-    for k in range(count):
-        mix_ref[k, pl.ds(feature_rows, unit), :] = part[k * unit : (k + 1) * unit]
+    nexts = [
+        jnp.concatenate([g[:, xs // 2 :], jnp.zeros((cout, xs // 2), BF16)], axis=1)
+        for g in grads
+    ]
+    none = jnp.zeros_like(grads[0])
+
+    def line(*pieces):
+        return jnp.concatenate(pieces, axis=1)
+
+    def stack(*pieces):
+        return jnp.concatenate(pieces, axis=0)
+
+    def taken(first, at):
+        return line(*[xx_vmem[z, pl.ds(at, third)] for z in range(first, planes, 2)])
+
+    for z in range(0, planes, 2):
+        copies[z].wait()
+    for z in range(1, planes, 2):
+        copies[z].start()
+    here = stack(line(none, *grads), line(*grads, none))
+    after = stack(line(none, *nexts), line(*nexts, none))
+    outer_two = dot_t(taken(0, third), stack(here, after))
+    outer_one = dot_t(taken(0, 0), here)
+    for z in range(1, planes, 2):
+        copies[z].wait()
+    inner_two = dot_t(taken(1, third), stack(line(*grads), line(*nexts)))
+    inner_one = dot_t(taken(1, 0), line(*grads))
+    part = stack(
+        outer_two[:, : 2 * cout],
+        outer_two[:, 2 * cout :],
+        outer_one,
+        inner_two,
+        line(inner_one[: third // 2], inner_one[third // 2 :]),
+        jnp.zeros((count * unit - 9 * third // 2, xs), F32),
+    )
+    part_vmem[...] = part.astype(BF16).reshape(count, unit, xs)
+    out = pltpu.make_async_copy(
+        part_vmem, mix_ref.at[:, pl.ds(slots * cout, unit)], sems.at[planes]
+    )
+    out.start()
+    out.wait()
 
 
 def sum_kernel(back_ref, total_ref, *, scale):
@@ -164,20 +227,25 @@
     for v in range(1, volumes):
         total = total + total_ref[v].astype(F32)
     total = total.reshape(count * unit, xs)
-    high = total[:rows]
-    low = total[rows : rows + rows // 2]
-    out_ref[2] = high[:, :cout]
-    out_ref[0] = high[:, cout:]
-    out_ref[1] = jnp.concatenate([low[:, :cout], low[:, cout:]], axis=0)
-
-
-def input_kernel(recv_ref, k_ref, out_ref, gg_ref, w_ref, t_ref):
+    third = rows // 3
+    for at, b in enumerate((2, 0, 1)):
+        piece = total[at * third : (at + 1) * third]
+        out_ref[2, pl.ds(b * third, third), :] = piece[:, :cout]
+        out_ref[0, pl.ds(b * third, third), :] = piece[:, cout:]
+    piece = total[3 * third : 4 * third]
+    out_ref[1, pl.ds(2 * third, third), :] = piece[:, :cout]
+    out_ref[1, pl.ds(0, third), :] = piece[:, cout:]
+    piece = total[4 * third : 4 * third + third // 2]
+    out_ref[1, pl.ds(third, third // 2), :] = piece[:, :cout]
+    out_ref[1, pl.ds(third + third // 2, third // 2), :] = piece[:, cout:]
+
+
+def input_kernel(recv_ref, halo_ref, k_ref, out_ref, gg_ref, w_ref, t_ref):
     cin, planes, ys, xs = out_ref.shape
     blocks, slots, cout, _ = recv_ref.shape
     shifts = shift_matrix(xs)
 
-    def shifted(p, carry):
-        here = recv_ref[:, p].reshape(blocks * cout, xs)
+    def shifted(p, here):
         after = jnp.concatenate([here[cout:], jnp.zeros((cout, xs), BF16)], axis=0)
         out = dot(jnp.concatenate([here, after], axis=1), shifts).astype(BF16)
         for k in range(blocks):
@@ -186,9 +254,10 @@
             gg_ref[p, pl.ds(0, cout), lanes] = here[rows]
             for v in range(1, 4):
                 gg_ref[p, pl.ds(v * cout, cout), lanes] = out[rows, (v - 1) * xs : v * xs]
-        return carry
-
-    lax.fori_loop(0, slots, shifted, 0)
+
+    for p in range(slots):
+        shifted(p, recv_ref[:, p].reshape(blocks * cout, xs))
+    shifted(slots, halo_ref[...].reshape(blocks * cout, xs))
     for zp in range(2):
         for yp in range(2):
             for xp in range(2):
@@ -231,13 +300,22 @@
     lax.fori_loop(0, planes // 2, one, 0)
 
 
-def call(kernel, outs, scratch=(), mib=24):
+def call(kernel, outs, scratch=(), mib=24, **kwargs):
     return pl.pallas_call(
         kernel,
         out_shape=outs,
         scratch_shapes=scratch,
         compiler_params=pltpu.CompilerParams(vmem_limit_bytes=mib << 20),
+        **kwargs,
     )
+
+
+def stay(value):
+    return pltpu.with_memory_space_constraint(value, pltpu.HBM)
+
+
+HBM = pl.BlockSpec(memory_space=pltpu.HBM)
+VMEM = pl.BlockSpec(memory_space=pltpu.VMEM)
 
 
 def shards(volume, kernel, cotangent):
@@ -248,34 +326,68 @@
     slots = planes // 2
     blocks = ys // 4
     lanes = blocks * xs
+    unit = -(-(27 * cin // 2) // (16 * blocks)) * 16
     taps = jnp.transpose(kernel, (2, 3, 4, 1, 0)).reshape(27, cin, cout)
 
-    grads = jnp.transpose(cotangent[0], (1, 0, 2, 3)).reshape(count, slots, cout, band * oxs)
-    above = jnp.concatenate([grads[1:, :1], jnp.zeros_like(grads[:1, :1])], axis=0)
-    packed = jnp.concatenate([grads, above], axis=1)
+    if band == 2:
+        packed, plane = call(
+            pack_kernel,
+            (
+                jax.ShapeDtypeStruct((count, slots, cout, xs), BF16),
+                jax.ShapeDtypeStruct((cin, ys, xs), BF16),
+            ),
+            (
+                pltpu.VMEM((4, cout * ozs * band // 4, oxs), BF16),
+                pltpu.VMEM((cout * ozs * band // 4, xs), F32),
+                pltpu.SemaphoreType.DMA((5,)),
+            ),
+            in_specs=(HBM, HBM),
+            out_specs=(VMEM, VMEM),
+        )(stay(cotangent.reshape(cout * ozs * band, oxs)), stay(volume[0]))
+    else:
+        packed = jnp.transpose(cotangent[0], (1, 0, 2, 3)).reshape(count, slots, cout, band * oxs)
+        plane = volume[0, :, planes - 1]
+    under = lax.ppermute(plane, "gz", [(i, i + 1) for i in range(count - 1)])
     recv = lax.all_to_all(packed, "gz", 0, 0, tiled=True)
     if band != 2:
-        recv = recv.reshape(blocks, 2, slots + 1, cout, oxs)
-        recv = jnp.transpose(recv, (0, 2, 3, 1, 4)).reshape(blocks, slots + 1, cout, xs)
-
-    xx, send = call(
+        recv = recv.reshape(blocks, 2 // band, slots, cout, band, oxs)
+        recv = jnp.transpose(recv, (0, 2, 3, 1, 4, 5)).reshape(blocks, slots, cout, xs)
+    above = lax.ppermute(recv[:, 0], "gz", [(i + 1, i) for i in range(count - 1)])
+
+    xx, mix = call(
         forward_kernel,
         (
-            jax.ShapeDtypeStruct((planes, 9 * cin, lanes), BF16),
-            jax.ShapeDtypeStruct((blocks, slots + 1, cout, xs), BF16),
+            pltpu.HBM((planes + 1, 6 * cin, lanes), BF16),
+            pltpu.HBM((blocks, slots * cout + unit, xs), BF16),
         ),
-        (pltpu.VMEM((cin * ys, xs), F32), pltpu.VMEM((2, blocks * cin, 2 * xs), BF16)),
-    )(volume[0], taps)
-    if band != 2:
-        send = send.reshape(blocks, slots + 1, cout, 2, oxs)
-        send = jnp.transpose(send, (0, 3, 1, 2, 4)).reshape(count, slots + 1, cout, band * oxs)
-        send = jnp.pad(send, ((0, 0), (0, 0), (0, 0), (0, xs - band * oxs)))
-    send = send.reshape(count, (slots + 1) * cout, xs)
-    unit = -(-(27 * cin // 2) // (16 * count)) * 16
+        (
+            pltpu.VMEM((planes + 1, 9 * cin, lanes), BF16),
+            pltpu.VMEM((cin * ys, xs), F32),
+            pltpu.VMEM((2, blocks * cin, 2 * xs), BF16),
+            pltpu.SemaphoreType.DMA((planes + 1,)),
+        ),
+        in_specs=(VMEM, VMEM, VMEM),
+        out_specs=(HBM, VMEM),
+    )(volume[0], under, taps)
     mix = call(
         weight_kernel,
-        jax.ShapeDtypeStruct((count, (slots + 1) * cout + unit, xs), BF16),
-    )(recv, xx, send)
+        pltpu.HBM(mix.shape, BF16),
+        (
+            pltpu.VMEM(xx.shape, BF16),
+            pltpu.VMEM((blocks, unit, xs), BF16),
+            pltpu.SemaphoreType.DMA((planes + 2,)),
+        ),
+        in_specs=(VMEM, HBM, HBM),
+        out_specs=HBM,
+        input_output_aliases={2: 0},
+    )(recv, stay(xx), stay(mix))
+    if band != 2:
+        send = mix[:, : slots * cout].reshape(blocks, slots * cout, 2 // band, band * oxs)
+        send = jnp.transpose(send, (0, 2, 1, 3)).reshape(count, slots * cout, band * oxs)
+        send = jnp.pad(send, ((0, 0), (0, 0), (0, xs - band * oxs)))
+        terms = mix[:, slots * cout :].reshape(count, blocks * unit // count, xs)
+        mix = jnp.concatenate([send, terms], axis=1)
+        unit = terms.shape[1]
     back = lax.all_to_all(mix, "gz", 0, 0, tiled=True)
     volumes = volume.shape[0] * lax.axis_size("vol")
 
@@ -284,12 +396,8 @@
 
     total = call(add, jax.ShapeDtypeStruct((everyone, unit, xs), BF16))(back)
     total = lax.all_to_all(total, ("vol", "gz"), 0, 0, tiled=True)
-    back = back[:, : (slots + 1) * cout].reshape(count, slots + 1, cout, xs)
-    carried = jnp.concatenate([jnp.zeros_like(back[:1, slots:]), back[:-1, slots:]], axis=0)
-    first = (back[:, :1].astype(F32) + carried.astype(F32)).astype(BF16)
-    whole = jnp.concatenate([first, back[:, 1:slots]], axis=1)
-    whole = whole[..., : band * oxs].reshape(ozs, cout, band, oxs)
-    features = jnp.transpose(whole, (1, 0, 2, 3))[None]
+    features = back[:, : slots * cout, : band * oxs].reshape(ozs, cout, band, oxs)
+    features = jnp.transpose(features, (1, 0, 2, 3))[None]
 
     volume_grad = call(
         input_kernel,
@@ -299,7 +407,7 @@
             pltpu.VMEM((8 * cin, 8 * cout), BF16),
             pltpu.VMEM((2, cin * ys, xs), F32),
         ),
-    )(recv, taps)[None]
+    )(recv, above, taps)[None]
 
     kernel_grad = call(final_kernel, jax.ShapeDtypeStruct((3, 9 * cin, cout), F32))(
         total.reshape(everyone // count, count, unit, xs)

time: 79.1 us -> 92.1 us (1.16)
  the two profiles are of different devices: /device:TPU:0 before, /device:TPU:11 now
where the time goes in v2:
time: 92.1 us; the launch traced here: 91.7 us
  Pallas kernels  26.2 us (28%)
  waiting for transfers between devices  22.5 us (24%)
  blocking collectives  22.5 us (24%)
  starting transfers between devices  17.1 us (19%)
  local copies, waits for them, and re-layouts  2.61 us (3%)
    all_to_all x1, blocking collectives, shards(): back = lax.all_to_all(mix, 'gz', 0, 0, tiled=True)  22.5 us
    ppermute x1, waiting for transfers between devices, shards(): under = lax.ppermute(plane, 'gz', [(i, i + 1) for i in range(count - 1)])  14.2 us
    pallas_call x1, Pallas kernels, shards(): call(forward_kernel, (pltpu.HBM((planes + 1, 6 * cin, lanes), BF16), pltp...  8.6 us
    ppermute x1, waiting for transfers between devices, shards(): lax.ppermute(recv[:, 0], 'gz', [(i + 1, i) for i in range(count - 1)])  8.32 us
    pallas_call x1, Pallas kernels, shards(): call(input_kernel, jax.ShapeDtypeStruct((cin, planes, ys, xs), BF16), (pl...  7.31 us
    all_to_all x1, starting transfers between devices, shards(): recv = lax.all_to_all(packed, 'gz', 0, 0, tiled=True)  6.53 us
    pallas_call x1, Pallas kernels, shards(): call(weight_kernel, pltpu.HBM(mix.shape, BF16), (pltpu.VMEM(xx.shape, BF1...  5.25 us
    all_to_all x1, starting transfers between devices, shards(): total = lax.all_to_all(total, ('vol', 'gz'), 0, 0, tiled=True)  4.87 us
  transfers between devices with their start and end apart: 4, of which 2 were waited for; matrix products, arithmetic and copies ran while one was open for 3% of the time, Pallas kernels for 17%

profile of v2, /device:TPU:11, one launch (start us, length us, event | category | flops | bytes accessed | tf_op | source)
XLA Modules:
  0.0 91.7 jit_solution(8986191236647013973)
XLA Ops:
  0.6 0.0 copy-start
  0.6 0.0 copy-start.1
  0.7 3.4 %shard_map.58 = (bf16[16,2,64,128]{3,2,1,0:T(8,128)(2,1)}, bf16[32,64,128]{2,1,0:T(8,128)(2,1)S(1)}) custom-call(bf16[4096,64]{1,0:T(8,128)(2,1)} %bitcast.25, bf16[32,4,64,128]{3,2,1,0:T(8,128)(2,1)} %bitcast.19), custom_call_target="tpu_custom_call" | custom-call | tf_op jit(solution)/shard_map/pallas_call | solution.py:333
  4.1 6.5 %all-to-all-start = ((bf16[16,2,64,128]{3,2,1,0:T(8,128)(2,1)}), bf16[16,2,64,128]{3,2,1,0:T(8,128)(2,1)S(1)}, u32[]{:S(2)}, u32[]{:S(2)}) async-start(bf16[16,2,64,128]{3,2,1,0:T(8,128)(2,1)} %get-tuple-element.7), calls=%async_computation | async-start | bytes 1048576 | tf_op jit(solution)/shard_map/all_to_all | solution.py:351
  10.6 3.4 %collective-permute-start = (bf16[32,64,128]{2,1,0:T(8,128)(2,1)S(1)}, bf16[32,64,128]{2,1,0:T(8,128)(2,1)S(1)}, u32[]{:S(2)}, u32[]{:S(2)}) collective-permute-start(bf16[32,64,128]{2,1,0:T(8,128)(2,1)S(1)} %get-tuple-element.8), channel_id=1, source_target_pairs={{0,1},{1,2},{2,3},{3,4},{4,5},{5,6},{6,7},{7,8},{8,9},{9,10},{10,1... | collective-permute-start | bytes 1572872 | tf_op jit(solution)/shard_map/ppermute | solution.py:350
  14.0 14.2 %collective-permute-done.halo_ref = bf16[32,64,128]{2,1,0:T(8,128)(2,1)S(1)} collective-permute-done((bf16[32,64,128]{2,1,0:T(8,128)(2,1)S(1)}, bf16[32,64,128]{2,1,0:T(8,128)(2,1)S(1)}, u32[]{:S(2)}, u32[]{:S(2)}) %collective-permute-start) | collective-permute-done | bytes 524320 | tf_op jit(solution)/shard_map/ppermute | solution.py:350
  28.2 0.0 copy-done
  28.2 0.0 copy-done.1
  28.2 8.6 %shard_map.59 = (bf16[5,192,2048]{2,1,0:T(8,128)(2,1)}, bf16[16,160,128]{2,1,0:T(8,128)(2,1)}) custom-call(bf16[32,4,64,128]{3,2,1,0:T(8,128)(2,1)S(1)} %bitcast.20, bf16[32,64,128]{2,1,0:T(8,128)(2,1)S(1)} %collective-permute-done.halo_ref, bf16[27,32,64]{2,1,0:T(8,128)(2,1)S(1)} %bitcast.22), custom_call_target="tpu_custom_call" | custom-call | tf_op jit(solution)/shard_map/pallas_call | solution.py:357
  36.8 0.0 all-to-all-done.recv_ref
  36.8 5.3 %shard_map.60 = bf16[16,160,128]{2,1,0:T(8,128)(2,1)} custom-call(bf16[16,2,64,128]{3,2,1,0:T(8,128)(2,1)S(1)} %all-to-all-done.recv_ref, bf16[5,192,2048]{2,1,0:T(8,128)(2,1)} %get-tuple-element.9.xx_ref, bf16[16,160,128]{2,1,0:T(8,128)(2,1)} %get-tuple-element.10.mix_in_ref), custom_call_target="tpu_custom_call", output_to_operand_aliasing={{}: (2, {})} | custom-call | tf_op jit(solution)/shard_map/pallas_call | solution.py:372
  42.1 22.5 %all_to_all.15.back_ref = bf16[16,160,128]{2,1,0:T(8,128)(2,1)S(1)} all-to-all(bf16[16,160,128]{2,1,0:T(8,128)(2,1)} %shard_map.60), channel_id=1, replica_groups=mesh['vol'=2,'gz'=16] {'gz'}, dimensions={0} | all-to-all | bytes 1310720 | tf_op jit(solution)/shard_map/all_to_all | solution.py:391
  64.6 0.7 shard_map.62
  65.3 4.9 %all-to-all-start.2 = ((bf16[32,32,128]{2,1,0:T(8,128)(2,1)}), bf16[32,32,128]{2,1,0:T(8,128)(2,1)S(1)}, u32[]{:S(2)}, u32[]{:S(2)}) async-start(bf16[32,32,128]{2,1,0:T(8,128)(2,1)} %shard_map.62), calls=%async_computation.2 | async-start | bytes 524288 | tf_op jit(solution)/shard_map/all_to_all | solution.py:398
  70.2 2.3 %collective-permute-start.1 = (bf16[16,64,128]{2,1,0:T(8,128)(2,1)S(1)}, bf16[16,64,128]{2,1,0:T(8,128)(2,1)S(1)}, u32[]{:S(2)}, u32[]{:S(2)}) collective-permute-start(bf16[16,64,128]{2,1,0:T(8,128)(2,1)S(1)} %slice_bitcast_fusion), channel_id=1, source_target_pairs={{1,0},{2,1},{3,2},{4,3},{5,4},{6,5},{7,6},{8,7},{9,8},{10,9},{11,1... | collective-permute-start | bytes 786440 | tf_op jit(solution)/shard_map/ppermute | solution.py:355
  72.5 8.3 %collective-permute-done.1.halo_ref = bf16[16,64,128]{2,1,0:T(8,128)(2,1)S(1)} collective-permute-done((bf16[16,64,128]{2,1,0:T(8,128)(2,1)S(1)}, bf16[16,64,128]{2,1,0:T(8,128)(2,1)S(1)}, u32[]{:S(2)}, u32[]{:S(2)}) %collective-permute-start.1) | collective-permute-done | bytes 262176 | tf_op jit(solution)/shard_map/ppermute | solution.py:355
  80.9 7.3 %shard_map.61 = bf16[32,4,64,128]{3,2,1,0:T(8,128)(2,1)} custom-call(bf16[16,2,64,128]{3,2,1,0:T(8,128)(2,1)S(1)} %all-to-all-done.recv_ref, bf16[16,64,128]{2,1,0:T(8,128)(2,1)S(1)} %collective-permute-done.1.halo_ref, bf16[27,32,64]{2,1,0:T(8,128)(2,1)S(1)} %bitcast.23), custom_call_target="tpu_custom_call" | custom-call | tf_op jit(solution)/shard_map/pallas_call | solution.py:402
  88.2 0.4 reshape.23
  88.6 2.1 %copy.15 = bf16[32,64,2,64]{3,2,0,1:T(2,128)(2,1)} copy(bf16[32,64,2,64]{3,2,1,0:T(2,128)(2,1)S(1)} %reshape.23) | data formatting | bytes 1048576 | tf_op jit(solution)/shard_map/reshape | solution.py:399
  90.8 0.0 all-to-all-done.2
  90.8 0.9 shard_map.63
  (2 shorter events, 0.1 us)
Async XLA Ops:
  0.6 27.5 %copy-start = (bf16[1,32,4,64,128]{4,3,2,1,0:T(8,128)(2,1)S(1)}, bf16[1,32,4,64,128]{4,3,2,1,0:T(8,128)(2,1)}, u32[]{:S(2)}) copy-start(bf16[1,32,4,64,128]{4,3,2,1,0:T(8,128)(2,1)} %param.3) | copy-start | bytes 6291460
  0.6 27.5 %copy-start.1 = (bf16[64,32,3,3,3]{0,1,4,3,2:T(8,128)(2,1)S(1)}, bf16[64,32,3,3,3]{0,1,4,3,2:T(8,128)(2,1)}, u32[]{:S(2)}) copy-start(bf16[64,32,3,3,3]{0,1,4,3,2:T(8,128)(2,1)} %param.4) | copy-start | bytes 331780
  4.1 32.7 %all-to-all-start = ((bf16[16,2,64,128]{3,2,1,0:T(8,128)(2,1)}), bf16[16,2,64,128]{3,2,1,0:T(8,128)(2,1)S(1)}, u32[]{:S(2)}, u32[]{:S(2)}) async-start(bf16[16,2,64,128]{3,2,1,0:T(8,128)(2,1)} %get-tuple-element.7), calls=%async_computation | async-start | bytes 1048576 | tf_op jit(solution)/shard_map/all_to_all | solution.py:351
  10.6 17.6 %collective-permute-start = (bf16[32,64,128]{2,1,0:T(8,128)(2,1)S(1)}, bf16[32,64,128]{2,1,0:T(8,128)(2,1)S(1)}, u32[]{:S(2)}, u32[]{:S(2)}) collective-permute-start(bf16[32,64,128]{2,1,0:T(8,128)(2,1)S(1)} %get-tuple-element.8), channel_id=1, source_target_pairs={{0,1},{1,2},{2,3},{3,4},{4,5},{5,6},{6,7},{7,8},{8,9},{9,10},{10,1... | collective-permute-start | bytes 1572872 | tf_op jit(solution)/shard_map/ppermute | solution.py:350
  65.3 25.4 %all-to-all-start.2 = ((bf16[32,32,128]{2,1,0:T(8,128)(2,1)}), bf16[32,32,128]{2,1,0:T(8,128)(2,1)S(1)}, u32[]{:S(2)}, u32[]{:S(2)}) async-start(bf16[32,32,128]{2,1,0:T(8,128)(2,1)} %shard_map.62), calls=%async_computation.2 | async-start | bytes 524288 | tf_op jit(solution)/shard_map/all_to_all | solution.py:398
  70.2 10.6 %collective-permute-start.1 = (bf16[16,64,128]{2,1,0:T(8,128)(2,1)S(1)}, bf16[16,64,128]{2,1,0:T(8,128)(2,1)S(1)}, u32[]{:S(2)}, u32[]{:S(2)}) collective-permute-start(bf16[16,64,128]{2,1,0:T(8,128)(2,1)S(1)} %slice_bitcast_fusion), channel_id=1, source_target_pairs={{1,0},{2,1},{3,2},{4,3},{5,4},{6,5},{7,6},{8,7},{9,8},{10,9},{11,1... | collective-permute-start | bytes 786440 | tf_op jit(solution)/shard_map/ppermute | solution.py:355

commit v3 on v2

--- a/solution.py
+++ b/solution.py
@@ -151,17 +151,12 @@
         leave(z).wait()
 
 
-def weight_kernel(recv_ref, xx_ref, mix_in_ref, mix_ref, xx_vmem, part_vmem, sems):
+def weight_kernel(recv_ref, xx_ref, mix_in_ref, mix_ref, part_vmem, sem):
     del mix_in_ref
     blocks, slots, cout, xs = recv_ref.shape
     planes, rows, _ = xx_ref.shape
     count, unit, _ = part_vmem.shape
-    copies = [
-        pltpu.make_async_copy(xx_ref.at[z], xx_vmem.at[z], sems.at[z]) for z in range(planes)
-    ]
     third = rows // 2
-    for z in range(0, planes, 2):
-        copies[z].start()
     grads = [
         jnp.concatenate([recv_ref[k, p] for k in range(blocks)], axis=1) for p in range(slots)
     ]
@@ -178,18 +173,12 @@
         return jnp.concatenate(pieces, axis=0)
 
     def taken(first, at):
-        return line(*[xx_vmem[z, pl.ds(at, third)] for z in range(first, planes, 2)])
-
-    for z in range(0, planes, 2):
-        copies[z].wait()
-    for z in range(1, planes, 2):
-        copies[z].start()
+        return line(*[xx_ref[z, pl.ds(at, third)] for z in range(first, planes, 2)])
+
     here = stack(line(none, *grads), line(*grads, none))
     after = stack(line(none, *nexts), line(*nexts, none))
     outer_two = dot_t(taken(0, third), stack(here, after))
     outer_one = dot_t(taken(0, 0), here)
-    for z in range(1, planes, 2):
-        copies[z].wait()
     inner_two = dot_t(taken(1, third), stack(line(*grads), line(*nexts)))
     inner_one = dot_t(taken(1, 0), line(*grads))
     part = stack(
@@ -202,7 +191,7 @@
     )
     part_vmem[...] = part.astype(BF16).reshape(count, unit, xs)
     out = pltpu.make_async_copy(
-        part_vmem, mix_ref.at[:, pl.ds(slots * cout, unit)], sems.at[planes]
+        part_vmem, mix_ref.at[:, pl.ds(slots * cout, unit)], sem
     )
     out.start()
     out.wait()
@@ -373,14 +362,13 @@
         weight_kernel,
         pltpu.HBM(mix.shape, BF16),
         (
-            pltpu.VMEM(xx.shape, BF16),
             pltpu.VMEM((blocks, unit, xs), BF16),
-            pltpu.SemaphoreType.DMA((planes + 2,)),
+            pltpu.SemaphoreType.DMA,
         ),
-        in_specs=(VMEM, HBM, HBM),
+        in_specs=(VMEM, VMEM, HBM),
         out_specs=HBM,
         input_output_aliases={2: 0},
-    )(recv, stay(xx), stay(mix))
+    )(recv, xx, stay(mix))
     if band != 2:
         send = mix[:, : slots * cout].reshape(blocks, slots * cout, 2 // band, band * oxs)
         send = jnp.transpose(send, (0, 2, 1, 3)).reshape(count, slots * cout, band * oxs)

time: 92.1 us -> 91.5 us (level)
  Pallas kernels: 26.2 us -> 23.5 us
  local copies, waits for them, and re-layouts: 2.61 us -> 4.72 us
    pallas_call x1, Pallas kernels: 5.25 us -> 2.49 us  [shards(): call(weight_kernel, pltpu.HBM(mix.shape, BF16), (pltpu.VMEM((blocks, unit...]
    unnamed x4 -> x6, local copies, waits for them, and re-layouts: 0.01 us -> 2.11 us
where the time goes in v3:
time: 91.5 us; the launch traced here: 91 us
  Pallas kernels  23.5 us (26%)
  waiting for transfers between devices  22.5 us (25%)
  blocking collectives  22.5 us (25%)
  starting transfers between devices  17.1 us (19%)
  local copies, waits for them, and re-layouts  4.72 us (5%)
    all_to_all x1, blocking collectives, shards(): back = lax.all_to_all(mix, 'gz', 0, 0, tiled=True)  22.5 us
    ppermute x1, waiting for transfers between devices, shards(): under = lax.ppermute(plane, 'gz', [(i, i + 1) for i in range(count - 1)])  14.2 us
    pallas_call x1, Pallas kernels, shards(): call(forward_kernel, (pltpu.HBM((planes + 1, 6 * cin, lanes), BF16), pltp...  8.6 us
    ppermute x1, waiting for transfers between devices, shards(): lax.ppermute(recv[:, 0], 'gz', [(i + 1, i) for i in range(count - 1)])  8.32 us
    pallas_call x1, Pallas kernels, shards(): call(input_kernel, jax.ShapeDtypeStruct((cin, planes, ys, xs), BF16), (pl...  7.31 us
    all_to_all x1, starting transfers between devices, shards(): recv = lax.all_to_all(packed, 'gz', 0, 0, tiled=True)  6.53 us
    all_to_all x1, starting transfers between devices, shards(): total = lax.all_to_all(total, ('vol', 'gz'), 0, 0, tiled=True)  4.87 us
    pallas_call x1, Pallas kernels, shards(): call(pack_kernel, (jax.ShapeDtypeStruct((count, slots, cout, xs), BF16),...  3.42 us
  transfers between devices with their start and end apart: 4, of which 2 were waited for; matrix products, arithmetic and copies ran while one was open for 3% of the time, Pallas kernels for 17%

profile of v3, /device:TPU:11, one launch (start us, length us, event | category | flops | bytes accessed | tf_op | source)
XLA Modules:
  0.0 91.0 jit_solution(16212745781105503547)
XLA Ops:
  0.6 0.0 copy-start
  0.6 0.0 copy-start.2
  0.7 3.4 %shard_map.58 = (bf16[16,2,64,128]{3,2,1,0:T(8,128)(2,1)}, bf16[32,64,128]{2,1,0:T(8,128)(2,1)S(1)}) custom-call(bf16[4096,64]{1,0:T(8,128)(2,1)} %bitcast.25, bf16[32,4,64,128]{3,2,1,0:T(8,128)(2,1)} %bitcast.19), custom_call_target="tpu_custom_call" | custom-call | tf_op jit(solution)/shard_map/pallas_call | solution.py:322
  4.1 6.5 %all-to-all-start = ((bf16[16,2,64,128]{3,2,1,0:T(8,128)(2,1)}), bf16[16,2,64,128]{3,2,1,0:T(8,128)(2,1)S(1)}, u32[]{:S(2)}, u32[]{:S(2)}) async-start(bf16[16,2,64,128]{3,2,1,0:T(8,128)(2,1)} %get-tuple-element.7), calls=%async_computation | async-start | bytes 1048576 | tf_op jit(solution)/shard_map/all_to_all | solution.py:340
  10.6 3.4 %collective-permute-start = (bf16[32,64,128]{2,1,0:T(8,128)(2,1)S(1)}, bf16[32,64,128]{2,1,0:T(8,128)(2,1)S(1)}, u32[]{:S(2)}, u32[]{:S(2)}) collective-permute-start(bf16[32,64,128]{2,1,0:T(8,128)(2,1)S(1)} %get-tuple-element.8), channel_id=1, source_target_pairs={{0,1},{1,2},{2,3},{3,4},{4,5},{5,6},{6,7},{7,8},{8,9},{9,10},{10,1... | collective-permute-start | bytes 1572872 | tf_op jit(solution)/shard_map/ppermute | solution.py:339
  14.0 14.2 %collective-permute-done.halo_ref = bf16[32,64,128]{2,1,0:T(8,128)(2,1)S(1)} collective-permute-done((bf16[32,64,128]{2,1,0:T(8,128)(2,1)S(1)}, bf16[32,64,128]{2,1,0:T(8,128)(2,1)S(1)}, u32[]{:S(2)}, u32[]{:S(2)}) %collective-permute-start) | collective-permute-done | bytes 524320 | tf_op jit(solution)/shard_map/ppermute | solution.py:339
  28.2 0.0 copy-done
  28.2 0.0 copy-done.2
  28.2 8.6 %shard_map.59 = (bf16[5,192,2048]{2,1,0:T(8,128)(2,1)}, bf16[16,160,128]{2,1,0:T(8,128)(2,1)}) custom-call(bf16[32,4,64,128]{3,2,1,0:T(8,128)(2,1)S(1)} %bitcast.20, bf16[32,64,128]{2,1,0:T(8,128)(2,1)S(1)} %collective-permute-done.halo_ref, bf16[27,32,64]{2,1,0:T(8,128)(2,1)S(1)} %bitcast.22), custom_call_target="tpu_custom_call" | custom-call | tf_op jit(solution)/shard_map/pallas_call | solution.py:346
  36.8 0.0 all-to-all-done.recv_ref
  36.8 0.0 copy-start.1
  36.8 2.1 %copy-done.1 = bf16[5,192,2048]{2,1,0:T(8,128)(2,1)S(1)} copy-done((bf16[5,192,2048]{2,1,0:T(8,128)(2,1)S(1)}, bf16[5,192,2048]{2,1,0:T(8,128)(2,1)}, u32[]{:S(2)}) %copy-start.1) | copy-done | bytes 3932184
  38.9 2.5 %shard_map.60 = bf16[16,160,128]{2,1,0:T(8,128)(2,1)} custom-call(bf16[16,2,64,128]{3,2,1,0:T(8,128)(2,1)S(1)} %all-to-all-done.recv_ref, bf16[5,192,2048]{2,1,0:T(8,128)(2,1)S(1)} %copy-done.1, bf16[16,160,128]{2,1,0:T(8,128)(2,1)} %get-tuple-element.10.mix_in_ref), custom_call_target="tpu_custom_call", output_to_operand_aliasing={{}: (2, {})} | custom-call | tf_op jit(solution)/shard_map/pallas_call | solution.py:361
  41.4 22.5 %all_to_all.15.back_ref = bf16[16,160,128]{2,1,0:T(8,128)(2,1)S(1)} all-to-all(bf16[16,160,128]{2,1,0:T(8,128)(2,1)} %shard_map.60), channel_id=1, replica_groups=mesh['vol'=2,'gz'=16] {'gz'}, dimensions={0} | all-to-all | bytes 1310720 | tf_op jit(solution)/shard_map/all_to_all | solution.py:379
  63.9 0.7 shard_map.62
  64.7 4.9 %all-to-all-start.2 = ((bf16[32,32,128]{2,1,0:T(8,128)(2,1)}), bf16[32,32,128]{2,1,0:T(8,128)(2,1)S(1)}, u32[]{:S(2)}, u32[]{:S(2)}) async-start(bf16[32,32,128]{2,1,0:T(8,128)(2,1)} %shard_map.62), calls=%async_computation.2 | async-start | bytes 524288 | tf_op jit(solution)/shard_map/all_to_all | solution.py:386
  69.6 2.3 %collective-permute-start.1 = (bf16[16,64,128]{2,1,0:T(8,128)(2,1)S(1)}, bf16[16,64,128]{2,1,0:T(8,128)(2,1)S(1)}, u32[]{:S(2)}, u32[]{:S(2)}) collective-permute-start(bf16[16,64,128]{2,1,0:T(8,128)(2,1)S(1)} %slice_bitcast_fusion), channel_id=1, source_target_pairs={{1,0},{2,1},{3,2},{4,3},{5,4},{6,5},{7,6},{8,7},{9,8},{10,9},{11,1... | collective-permute-start | bytes 786440 | tf_op jit(solution)/shard_map/ppermute | solution.py:344
  71.9 8.3 %collective-permute-done.1.halo_ref = bf16[16,64,128]{2,1,0:T(8,128)(2,1)S(1)} collective-permute-done((bf16[16,64,128]{2,1,0:T(8,128)(2,1)S(1)}, bf16[16,64,128]{2,1,0:T(8,128)(2,1)S(1)}, u32[]{:S(2)}, u32[]{:S(2)}) %collective-permute-start.1) | collective-permute-done | bytes 262176 | tf_op jit(solution)/shard_map/ppermute | solution.py:344
  80.2 7.3 %shard_map.61 = bf16[32,4,64,128]{3,2,1,0:T(8,128)(2,1)} custom-call(bf16[16,2,64,128]{3,2,1,0:T(8,128)(2,1)S(1)} %all-to-all-done.recv_ref, bf16[16,64,128]{2,1,0:T(8,128)(2,1)S(1)} %collective-permute-done.1.halo_ref, bf16[27,32,64]{2,1,0:T(8,128)(2,1)S(1)} %bitcast.23), custom_call_target="tpu_custom_call" | custom-call | tf_op jit(solution)/shard_map/pallas_call | solution.py:390
  87.6 0.4 reshape.23
  88.0 2.1 %copy.15 = bf16[32,64,2,64]{3,2,0,1:T(2,128)(2,1)} copy(bf16[32,64,2,64]{3,2,1,0:T(2,128)(2,1)S(1)} %reshape.23) | data formatting | bytes 1048576 | tf_op jit(solution)/shard_map/reshape | solution.py:387
  90.1 0.0 all-to-all-done.2
  90.1 0.9 shard_map.63
  (2 shorter events, 0.1 us)
Async XLA Ops:
  0.6 27.5 %copy-start = (bf16[1,32,4,64,128]{4,3,2,1,0:T(8,128)(2,1)S(1)}, bf16[1,32,4,64,128]{4,3,2,1,0:T(8,128)(2,1)}, u32[]{:S(2)}) copy-start(bf16[1,32,4,64,128]{4,3,2,1,0:T(8,128)(2,1)} %param.3) | copy-start | bytes 6291460
  0.6 27.5 %copy-start.2 = (bf16[64,32,3,3,3]{0,1,4,3,2:T(8,128)(2,1)S(1)}, bf16[64,32,3,3,3]{0,1,4,3,2:T(8,128)(2,1)}, u32[]{:S(2)}) copy-start(bf16[64,32,3,3,3]{0,1,4,3,2:T(8,128)(2,1)} %param.4) | copy-start | bytes 331780
  4.1 32.7 %all-to-all-start = ((bf16[16,2,64,128]{3,2,1,0:T(8,128)(2,1)}), bf16[16,2,64,128]{3,2,1,0:T(8,128)(2,1)S(1)}, u32[]{:S(2)}, u32[]{:S(2)}) async-start(bf16[16,2,64,128]{3,2,1,0:T(8,128)(2,1)} %get-tuple-element.7), calls=%async_computation | async-start | bytes 1048576 | tf_op jit(solution)/shard_map/all_to_all | solution.py:340
  10.6 17.6 %collective-permute-start = (bf16[32,64,128]{2,1,0:T(8,128)(2,1)S(1)}, bf16[32,64,128]{2,1,0:T(8,128)(2,1)S(1)}, u32[]{:S(2)}, u32[]{:S(2)}) collective-permute-start(bf16[32,64,128]{2,1,0:T(8,128)(2,1)S(1)} %get-tuple-element.8), channel_id=1, source_target_pairs={{0,1},{1,2},{2,3},{3,4},{4,5},{5,6},{6,7},{7,8},{8,9},{9,10},{10,1... | collective-permute-start | bytes 1572872 | tf_op jit(solution)/shard_map/ppermute | solution.py:339
  36.8 2.1 %copy-start.1 = (bf16[5,192,2048]{2,1,0:T(8,128)(2,1)S(1)}, bf16[5,192,2048]{2,1,0:T(8,128)(2,1)}, u32[]{:S(2)}) copy-start(bf16[5,192,2048]{2,1,0:T(8,128)(2,1)} %get-tuple-element.9.xx_ref) | copy-start | bytes 11796484
  64.7 25.4 %all-to-all-start.2 = ((bf16[32,32,128]{2,1,0:T(8,128)(2,1)}), bf16[32,32,128]{2,1,0:T(8,128)(2,1)S(1)}, u32[]{:S(2)}, u32[]{:S(2)}) async-start(bf16[32,32,128]{2,1,0:T(8,128)(2,1)} %shard_map.62), calls=%async_computation.2 | async-start | bytes 524288 | tf_op jit(solution)/shard_map/all_to_all | solution.py:386
  69.6 10.6 %collective-permute-start.1 = (bf16[16,64,128]{2,1,0:T(8,128)(2,1)S(1)}, bf16[16,64,128]{2,1,0:T(8,128)(2,1)S(1)}, u32[]{:S(2)}, u32[]{:S(2)}) collective-permute-start(bf16[16,64,128]{2,1,0:T(8,128)(2,1)S(1)} %slice_bitcast_fusion), channel_id=1, source_target_pairs={{1,0},{2,1},{3,2},{4,3},{5,4},{6,5},{7,6},{8,7},{9,8},{10,9},{11,1... | collective-permute-start | bytes 786440 | tf_op jit(solution)/shard_map/ppermute | solution.py:344

commit v4 on v3

--- a/solution.py
+++ b/solution.py
@@ -229,9 +229,21 @@
     out_ref[1, pl.ds(third + third // 2, third // 2), :] = piece[:, cout:]
 
 
-def input_kernel(recv_ref, halo_ref, k_ref, out_ref, gg_ref, w_ref, t_ref):
+def near_kernel(recv_ref, k_ref, out_ref, edge_ref, gg_ref, w_ref, t_ref):
+    edge_ref[...] = recv_ref[:, 0]
+    grads = [recv_ref[:, p] for p in range(recv_ref.shape[1])]
+    input_kernel(grads, k_ref, out_ref, gg_ref, w_ref, t_ref)
+
+
+def far_kernel(recv_ref, halo_ref, k_ref, out_in_ref, out_ref, gg_ref, w_ref, t_ref):
+    del out_in_ref
+    grads = [recv_ref[:, recv_ref.shape[1] - 1], halo_ref[...]]
+    input_kernel(grads, k_ref, out_ref, gg_ref, w_ref, t_ref)
+
+
+def input_kernel(grads, k_ref, out_ref, gg_ref, w_ref, t_ref):
     cin, planes, ys, xs = out_ref.shape
-    blocks, slots, cout, _ = recv_ref.shape
+    blocks, cout, _ = grads[0].shape
     shifts = shift_matrix(xs)
 
     def shifted(p, here):
@@ -244,9 +256,8 @@
             for v in range(1, 4):
                 gg_ref[p, pl.ds(v * cout, cout), lanes] = out[rows, (v - 1) * xs : v * xs]
 
-    for p in range(slots):
-        shifted(p, recv_ref[:, p].reshape(blocks * cout, xs))
-    shifted(slots, halo_ref[...].reshape(blocks * cout, xs))
+    for p, plane in enumerate(grads):
+        shifted(p, plane.reshape(blocks * cout, xs))
     for zp in range(2):
         for yp in range(2):
             for xp in range(2):
@@ -341,8 +352,6 @@
     if band != 2:
         recv = recv.reshape(blocks, 2 // band, slots, cout, band, oxs)
         recv = jnp.transpose(recv, (0, 2, 3, 1, 4, 5)).reshape(blocks, slots, cout, xs)
-    above = lax.ppermute(recv[:, 0], "gz", [(i + 1, i) for i in range(count - 1)])
-
     xx, mix = call(
         forward_kernel,
         (
@@ -387,15 +396,35 @@
     features = back[:, : slots * cout, : band * oxs].reshape(ozs, cout, band, oxs)
     features = jnp.transpose(features, (1, 0, 2, 3))[None]
 
-    volume_grad = call(
-        input_kernel,
-        jax.ShapeDtypeStruct((cin, planes, ys, xs), BF16),
-        (
-            pltpu.VMEM((slots + 1, 4 * cout, lanes), BF16),
+    def scratch(slabs):
+        return (
+            pltpu.VMEM((slabs + 1, 4 * cout, lanes), BF16),
             pltpu.VMEM((8 * cin, 8 * cout), BF16),
             pltpu.VMEM((2, cin * ys, xs), F32),
+        )
+
+    whole = pltpu.HBM((cin, planes, ys, xs), BF16)
+    volume_grad, edge = call(
+        near_kernel,
+        (whole, pltpu.HBM((blocks, cout, xs), BF16)),
+        scratch(slots - 1),
+        grid=(1,),
+        in_specs=(VMEM, VMEM),
+        out_specs=(
+            pl.BlockSpec((cin, planes - 2, ys, xs), lambda i: (0, 0, 0, 0)),
+            VMEM,
         ),
-    )(recv, above, taps)[None]
+    )(recv, taps)
+    above = lax.ppermute(edge, "gz", [(i + 1, i) for i in range(count - 1)])
+    volume_grad = call(
+        far_kernel,
+        whole,
+        scratch(1),
+        grid=(1,),
+        in_specs=(VMEM, VMEM, VMEM, HBM),
+        out_specs=pl.BlockSpec((cin, 2, ys, xs), lambda i: (0, slots - 1, 0, 0)),
+        input_output_aliases={3: 0},
+    )(recv, above, taps, stay(volume_grad))[None]
 
     kernel_grad = call(final_kernel, jax.ShapeDtypeStruct((3, 9 * cin, cout), F32))(
         total.reshape(everyone // count, count, unit, xs)

time: 91.5 us -> 90.5 us (0.989)
  the two profiles are of different devices: /device:TPU:11 before, /device:TPU:3 now
where the time goes in v4:
time: 90.5 us; the launch traced here: 90 us
  blocking collectives  25.4 us (28%)
  Pallas kernels  24.2 us (27%)
  waiting for transfers between devices  18.4 us (20%)
  starting transfers between devices  16.6 us (18%)
  local copies, waits for them, and re-layouts  4.7 us (5%)
    all_to_all x1, blocking collectives, shards(): back = lax.all_to_all(mix, 'gz', 0, 0, tiled=True)  25.4 us
    ppermute x1, waiting for transfers between devices, shards(): under = lax.ppermute(plane, 'gz', [(i, i + 1) for i in range(count - 1)])  12.1 us
    pallas_call x1, Pallas kernels, shards(): call(forward_kernel, (pltpu.HBM((planes + 1, 6 * cin, lanes), BF16), pltp...  8.6 us
    all_to_all x1, starting transfers between devices, shards(): recv = lax.all_to_all(packed, 'gz', 0, 0, tiled=True)  6.65 us
    ppermute x1, waiting for transfers between devices, shards(): above = lax.ppermute(edge, 'gz', [(i + 1, i) for i in range(count - 1)])  6.31 us
    all_to_all x1, starting transfers between devices, shards(): total = lax.all_to_all(total, ('vol', 'gz'), 0, 0, tiled=True)  4.14 us
    pallas_call x1, Pallas kernels, shards(): call(near_kernel, (whole, pltpu.HBM((blocks, cout, xs), BF16)), scratch(s...  4.09 us
    pallas_call x1, Pallas kernels, shards(): call(far_kernel, whole, scratch(1), grid=(1,), in_specs=(VMEM, VMEM, VMEM...  4 us
  transfers between devices with their start and end apart: 4, of which 2 were waited for; matrix products, arithmetic and copies ran while one was open for 3% of the time, Pallas kernels for 19%

profile of v4, /device:TPU:3, one launch (start us, length us, event | category | flops | bytes accessed | tf_op | source)
XLA Modules:
  0.0 90.0 jit_solution(12995467550994231647)
XLA Ops:
  0.6 0.0 copy-start
  0.6 0.0 copy-start.2
  0.7 3.4 %shard_map.58 = (bf16[16,2,64,128]{3,2,1,0:T(8,128)(2,1)}, bf16[32,64,128]{2,1,0:T(8,128)(2,1)S(1)}) custom-call(bf16[4096,64]{1,0:T(8,128)(2,1)} %bitcast.22, bf16[32,4,64,128]{3,2,1,0:T(8,128)(2,1)} %bitcast.15), custom_call_target="tpu_custom_call" | custom-call | tf_op jit(solution)/shard_map/pallas_call | solution.py:333
  4.1 6.6 %all-to-all-start = ((bf16[16,2,64,128]{3,2,1,0:T(8,128)(2,1)}), bf16[16,2,64,128]{3,2,1,0:T(8,128)(2,1)S(1)}, u32[]{:S(2)}, u32[]{:S(2)}) async-start(bf16[16,2,64,128]{3,2,1,0:T(8,128)(2,1)} %get-tuple-element.9), calls=%async_computation | async-start | bytes 1048576 | tf_op jit(solution)/shard_map/all_to_all | solution.py:351
  10.7 3.4 %collective-permute-start = (bf16[32,64,128]{2,1,0:T(8,128)(2,1)S(1)}, bf16[32,64,128]{2,1,0:T(8,128)(2,1)S(1)}, u32[]{:S(2)}, u32[]{:S(2)}) collective-permute-start(bf16[32,64,128]{2,1,0:T(8,128)(2,1)S(1)} %get-tuple-element.10), channel_id=1, source_target_pairs={{0,1},{1,2},{2,3},{3,4},{4,5},{5,6},{6,7},{7,8},{8,9},{9,10},{10,1... | collective-permute-start | bytes 1572872 | tf_op jit(solution)/shard_map/ppermute | solution.py:350
  14.1 12.1 %collective-permute-done.halo_ref = bf16[32,64,128]{2,1,0:T(8,128)(2,1)S(1)} collective-permute-done((bf16[32,64,128]{2,1,0:T(8,128)(2,1)S(1)}, bf16[32,64,128]{2,1,0:T(8,128)(2,1)S(1)}, u32[]{:S(2)}, u32[]{:S(2)}) %collective-permute-start) | collective-permute-done | bytes 524320 | tf_op jit(solution)/shard_map/ppermute | solution.py:350
  26.2 0.0 copy-done
  26.2 0.0 copy-done.2
  26.2 8.6 %shard_map.59 = (bf16[5,192,2048]{2,1,0:T(8,128)(2,1)}, bf16[16,160,128]{2,1,0:T(8,128)(2,1)}) custom-call(bf16[32,4,64,128]{3,2,1,0:T(8,128)(2,1)S(1)} %bitcast.16, bf16[32,64,128]{2,1,0:T(8,128)(2,1)S(1)} %collective-permute-done.halo_ref, bf16[27,32,64]{2,1,0:T(8,128)(2,1)S(1)} %bitcast.17), custom_call_target="tpu_custom_call" | custom-call | tf_op jit(solution)/shard_map/pallas_call | solution.py:355
  34.8 0.0 all-to-all-done.recv_ref
  34.8 0.0 copy-start.1
  34.8 2.1 %copy-done.1 = bf16[5,192,2048]{2,1,0:T(8,128)(2,1)S(1)} copy-done((bf16[5,192,2048]{2,1,0:T(8,128)(2,1)S(1)}, bf16[5,192,2048]{2,1,0:T(8,128)(2,1)}, u32[]{:S(2)}) %copy-start.1) | copy-done | bytes 3932184
  36.9 2.5 %shard_map.60 = bf16[16,160,128]{2,1,0:T(8,128)(2,1)} custom-call(bf16[16,2,64,128]{3,2,1,0:T(8,128)(2,1)S(1)} %all-to-all-done.recv_ref, bf16[5,192,2048]{2,1,0:T(8,128)(2,1)S(1)} %copy-done.1, bf16[16,160,128]{2,1,0:T(8,128)(2,1)} %get-tuple-element.12.mix_in_ref), custom_call_target="tpu_custom_call", output_to_operand_aliasing={{}: (2, {})} | custom-call | tf_op jit(solution)/shard_map/pallas_call | solution.py:370
  39.4 25.4 %all_to_all.15.back_ref = bf16[16,160,128]{2,1,0:T(8,128)(2,1)S(1)} all-to-all(bf16[16,160,128]{2,1,0:T(8,128)(2,1)} %shard_map.60), channel_id=1, replica_groups=mesh['vol'=2,'gz'=16] {'gz'}, dimensions={0} | all-to-all | bytes 1310720 | tf_op jit(solution)/shard_map/all_to_all | solution.py:388
  64.8 0.7 shard_map.63
  65.5 4.1 %all-to-all-start.2 = ((bf16[32,32,128]{2,1,0:T(8,128)(2,1)}), bf16[32,32,128]{2,1,0:T(8,128)(2,1)S(1)}, u32[]{:S(2)}, u32[]{:S(2)}) async-start(bf16[32,32,128]{2,1,0:T(8,128)(2,1)} %shard_map.63), calls=%async_computation.2 | async-start | bytes 524288 | tf_op jit(solution)/shard_map/all_to_all | solution.py:395
  69.7 4.1 %shard_map.61 = (bf16[32,4,64,128]{3,2,1,0:T(8,128)(2,1)}, bf16[16,64,128]{2,1,0:T(8,128)(2,1)}) custom-call(bf16[16,2,64,128]{3,2,1,0:T(8,128)(2,1)S(1)} %all-to-all-done.recv_ref, bf16[27,32,64]{2,1,0:T(8,128)(2,1)S(1)} %bitcast.18), custom_call_target="tpu_custom_call" | custom-call | tf_op jit(solution)/shard_map/pallas_call | solution.py:407
  73.8 2.5 %collective-permute-start.1 = (bf16[16,64,128]{2,1,0:T(8,128)(2,1)}, bf16[16,64,128]{2,1,0:T(8,128)(2,1)S(1)}, u32[]{:S(2)}, u32[]{:S(2)}) collective-permute-start(bf16[16,64,128]{2,1,0:T(8,128)(2,1)} %get-tuple-element.13), channel_id=1, source_target_pairs={{1,0},{2,1},{3,2},{4,3},{5,4},{6,5},{7,6},{8,7},{9,8},{10,9},{11,1... | collective-permute-start | bytes 786440 | tf_op jit(solution)/shard_map/ppermute | solution.py:418
  76.2 6.3 %collective-permute-done.1.halo_ref = bf16[16,64,128]{2,1,0:T(8,128)(2,1)S(1)} collective-permute-done((bf16[16,64,128]{2,1,0:T(8,128)(2,1)}, bf16[16,64,128]{2,1,0:T(8,128)(2,1)S(1)}, u32[]{:S(2)}, u32[]{:S(2)}) %collective-permute-start.1) | collective-permute-done | bytes 262176 | tf_op jit(solution)/shard_map/ppermute | solution.py:418
  82.5 4.0 %shard_map.62 = bf16[32,4,64,128]{3,2,1,0:T(8,128)(2,1)} custom-call(bf16[16,2,64,128]{3,2,1,0:T(8,128)(2,1)S(1)} %all-to-all-done.recv_ref, bf16[16,64,128]{2,1,0:T(8,128)(2,1)S(1)} %collective-permute-done.1.halo_ref, bf16[27,32,64]{2,1,0:T(8,128)(2,1)S(1)} %bitcast.19, ...), custom_call_target="tpu_custom_call", output_to_operand_aliasing={{}: (3, {})} | custom-call | tf_op jit(solution)/shard_map/pallas_call | solution.py:419
  86.6 0.4 reshape.23
  87.0 2.1 %copy.10 = bf16[32,64,2,64]{3,2,0,1:T(2,128)(2,1)} copy(bf16[32,64,2,64]{3,2,1,0:T(2,128)(2,1)S(1)} %reshape.23) | data formatting | bytes 1048576 | tf_op jit(solution)/shard_map/reshape | solution.py:396
  89.1 0.0 all-to-all-done.2
  89.2 0.9 shard_map.64
  (1 shorter events, 0.0 us)
Async XLA Ops:
  0.6 25.5 %copy-start = (bf16[1,32,4,64,128]{4,3,2,1,0:T(8,128)(2,1)S(1)}, bf16[1,32,4,64,128]{4,3,2,1,0:T(8,128)(2,1)}, u32[]{:S(2)}) copy-start(bf16[1,32,4,64,128]{4,3,2,1,0:T(8,128)(2,1)} %param.3) | copy-start | bytes 6291460
  0.6 25.5 %copy-start.2 = (bf16[64,32,3,3,3]{0,1,4,3,2:T(8,128)(2,1)S(1)}, bf16[64,32,3,3,3]{0,1,4,3,2:T(8,128)(2,1)}, u32[]{:S(2)}) copy-start(bf16[64,32,3,3,3]{0,1,4,3,2:T(8,128)(2,1)} %param.4) | copy-start | bytes 331780
  4.1 30.7 %all-to-all-start = ((bf16[16,2,64,128]{3,2,1,0:T(8,128)(2,1)}), bf16[16,2,64,128]{3,2,1,0:T(8,128)(2,1)S(1)}, u32[]{:S(2)}, u32[]{:S(2)}) async-start(bf16[16,2,64,128]{3,2,1,0:T(8,128)(2,1)} %get-tuple-element.9), calls=%async_computation | async-start | bytes 1048576 | tf_op jit(solution)/shard_map/all_to_all | solution.py:351
  10.7 15.4 %collective-permute-start = (bf16[32,64,128]{2,1,0:T(8,128)(2,1)S(1)}, bf16[32,64,128]{2,1,0:T(8,128)(2,1)S(1)}, u32[]{:S(2)}, u32[]{:S(2)}) collective-permute-start(bf16[32,64,128]{2,1,0:T(8,128)(2,1)S(1)} %get-tuple-element.10), channel_id=1, source_target_pairs={{0,1},{1,2},{2,3},{3,4},{4,5},{5,6},{6,7},{7,8},{8,9},{9,10},{10,1... | collective-permute-start | bytes 1572872 | tf_op jit(solution)/shard_map/ppermute | solution.py:350
  34.8 2.1 %copy-start.1 = (bf16[5,192,2048]{2,1,0:T(8,128)(2,1)S(1)}, bf16[5,192,2048]{2,1,0:T(8,128)(2,1)}, u32[]{:S(2)}) copy-start(bf16[5,192,2048]{2,1,0:T(8,128)(2,1)} %get-tuple-element.11.xx_ref) | copy-start | bytes 11796484
  65.5 23.6 %all-to-all-start.2 = ((bf16[32,32,128]{2,1,0:T(8,128)(2,1)}), bf16[32,32,128]{2,1,0:T(8,128)(2,1)S(1)}, u32[]{:S(2)}, u32[]{:S(2)}) async-start(bf16[32,32,128]{2,1,0:T(8,128)(2,1)} %shard_map.63), calls=%async_computation.2 | async-start | bytes 524288 | tf_op jit(solution)/shard_map/all_to_all | solution.py:395
  73.8 8.8 %collective-permute-start.1 = (bf16[16,64,128]{2,1,0:T(8,128)(2,1)}, bf16[16,64,128]{2,1,0:T(8,128)(2,1)S(1)}, u32[]{:S(2)}, u32[]{:S(2)}) collective-permute-start(bf16[16,64,128]{2,1,0:T(8,128)(2,1)} %get-tuple-element.13), channel_id=1, source_target_pairs={{1,0},{2,1},{3,2},{4,3},{5,4},{6,5},{7,6},{8,7},{9,8},{10,9},{11,1... | collective-permute-start | bytes 786440 | tf_op jit(solution)/shard_map/ppermute | solution.py:418

commit v5 on v4

--- a/solution.py
+++ b/solution.py
@@ -62,10 +62,11 @@
     return jnp.concatenate([k_ref[at + 2], k_ref[at]], axis=1)
 
 
-def pack_kernel(cot_ref, vol_ref, packed_ref, plane_ref, c_ref, s_ref, sems):
+def pack_kernel(cot_ref, vol_ref, sent_ref, plane_ref, c_ref, s_ref, packed_ref, v_ref, sems):
     parts = c_ref.shape[0]
-    copy = pltpu.make_async_copy(vol_ref.at[:, vol_ref.shape[1] - 1], plane_ref, sems.at[parts])
-    copy.start()
+    take = pltpu.make_async_copy(vol_ref.at[:, vol_ref.shape[1] - 1], v_ref, sems.at[parts])
+    give = pltpu.make_async_copy(v_ref, plane_ref, sems.at[parts + 1])
+    take.start()
     size = cot_ref.shape[0] // parts
     loads = [
         pltpu.make_async_copy(cot_ref.at[pl.ds(i * size, size)], c_ref.at[i], sems.at[i])
@@ -78,6 +79,14 @@
     own = cout // parts
     stride = size // own
     left = iota((own, xs), 1) < half
+    leaves = [
+        pltpu.make_async_copy(
+            packed_ref.at[:, :, pl.ds(i * own, own)],
+            sent_ref.at[:, :, pl.ds(i * own, own)],
+            sems.at[parts + 2 + i],
+        )
+        for i in range(parts)
+    ]
     for i in range(parts):
         loads[i].wait()
         s_ref[:, :half] = c_ref[i].astype(F32)
@@ -86,7 +95,13 @@
             high = s_ref[pl.ds(2 * p + 1, own, stride=stride), :]
             both = jnp.where(left, low, pltpu.roll(high, half, axis=1))
             packed_ref[p // slots, p % slots, pl.ds(i * own, own)] = both.astype(BF16)
-    copy.wait()
+        leaves[i].start()
+        if i == 0:
+            take.wait()
+            give.start()
+    for leave in leaves:
+        leave.wait()
+    give.wait()
 
 
 def forward_kernel(vol_ref, halo_ref, k_ref, out_ref, mix_ref, xx_ref, t_ref, x_ref, sems):
@@ -151,7 +166,7 @@
         leave(z).wait()
 
 
-def weight_kernel(recv_ref, xx_ref, mix_in_ref, mix_ref, part_vmem, sem):
+def weight_kernel(recv_ref, xx_ref, mix_in_ref, mix_ref, part_vmem, sems):
     del mix_in_ref
     blocks, slots, cout, xs = recv_ref.shape
     planes, rows, _ = xx_ref.shape
@@ -179,22 +194,31 @@
     after = stack(line(none, *nexts), line(*nexts, none))
     outer_two = dot_t(taken(0, third), stack(here, after))
     outer_one = dot_t(taken(0, 0), here)
+    outer = stack(outer_two[:, : 2 * cout], outer_two[:, 2 * cout :], outer_one).astype(BF16)
+    early = rows * 3 // 2 // unit
+    ahead = early * unit
+
+    def leave(first, last, sem):
+        return pltpu.make_async_copy(
+            part_vmem.at[pl.ds(first, last - first)],
+            mix_ref.at[pl.ds(first, last - first), pl.ds(slots * cout, unit)],
+            sem,
+        )
+
+    part_vmem[pl.ds(0, early)] = outer[:ahead].reshape(early, unit, xs)
+    leave(0, early, sems.at[0]).start()
     inner_two = dot_t(taken(1, third), stack(line(*grads), line(*nexts)))
     inner_one = dot_t(taken(1, 0), line(*grads))
     part = stack(
-        outer_two[:, : 2 * cout],
-        outer_two[:, 2 * cout :],
-        outer_one,
         inner_two,
         line(inner_one[: third // 2], inner_one[third // 2 :]),
         jnp.zeros((count * unit - 9 * third // 2, xs), F32),
-    )
-    part_vmem[...] = part.astype(BF16).reshape(count, unit, xs)
-    out = pltpu.make_async_copy(
-        part_vmem, mix_ref.at[:, pl.ds(slots * cout, unit)], sem
-    )
-    out.start()
-    out.wait()
+    ).astype(BF16)
+    part = stack(outer[ahead:], part) if ahead < 3 * third else part
+    part_vmem[pl.ds(early, count - early)] = part.reshape(count - early, unit, xs)
+    leave(early, count, sems.at[1]).start()
+    leave(0, early, sems.at[0]).wait()
+    leave(early, count, sems.at[1]).wait()
 
 
 def sum_kernel(back_ref, total_ref, *, scale):
@@ -333,16 +357,18 @@
         packed, plane = call(
             pack_kernel,
             (
-                jax.ShapeDtypeStruct((count, slots, cout, xs), BF16),
-                jax.ShapeDtypeStruct((cin, ys, xs), BF16),
+                pltpu.HBM((count, slots, cout, xs), BF16),
+                pltpu.HBM((cin, ys, xs), BF16),
             ),
             (
                 pltpu.VMEM((4, cout * ozs * band // 4, oxs), BF16),
                 pltpu.VMEM((cout * ozs * band // 4, xs), F32),
-                pltpu.SemaphoreType.DMA((5,)),
+                pltpu.VMEM((count, slots, cout, xs), BF16),
+                pltpu.VMEM((cin, ys, xs), BF16),
+                pltpu.SemaphoreType.DMA((10,)),
             ),
             in_specs=(HBM, HBM),
-            out_specs=(VMEM, VMEM),
+            out_specs=(HBM, HBM),
         )(stay(cotangent.reshape(cout * ozs * band, oxs)), stay(volume[0]))
     else:
         packed = jnp.transpose(cotangent[0], (1, 0, 2, 3)).reshape(count, slots, cout, band * oxs)
@@ -372,7 +398,7 @@
         pltpu.HBM(mix.shape, BF16),
         (
             pltpu.VMEM((blocks, unit, xs), BF16),
-            pltpu.SemaphoreType.DMA,
+            pltpu.SemaphoreType.DMA((2,)),
         ),
         in_specs=(VMEM, VMEM, HBM),
         out_specs=HBM,

time: 90.5 us -> 90.4 us (level)
  no operation moved by 1% of the time
where the time goes in v5:
time: 90.4 us; the launch traced here: 89.9 us
  blocking collectives  25.3 us (28%)
  Pallas kernels  24.1 us (27%)
  waiting for transfers between devices  18.5 us (20%)
  starting transfers between devices  16.6 us (18%)
  local copies, waits for them, and re-layouts  4.7 us (5%)
    all_to_all x1, blocking collectives, shards(): back = lax.all_to_all(mix, 'gz', 0, 0, tiled=True)  25.3 us
    ppermute x1, waiting for transfers between devices, shards(): under = lax.ppermute(plane, 'gz', [(i, i + 1) for i in range(count - 1)])  12.2 us
    pallas_call x1, Pallas kernels, shards(): call(forward_kernel, (pltpu.HBM((planes + 1, 6 * cin, lanes), BF16), pltp...  8.6 us
    all_to_all x1, starting transfers between devices, shards(): recv = lax.all_to_all(packed, 'gz', 0, 0, tiled=True)  6.65 us
    ppermute x1, waiting for transfers between devices, shards(): above = lax.ppermute(edge, 'gz', [(i + 1, i) for i in range(count - 1)])  6.32 us
    all_to_all x1, starting transfers between devices, shards(): total = lax.all_to_all(total, ('vol', 'gz'), 0, 0, tiled=True)  4.14 us
    pallas_call x1, Pallas kernels, shards(): call(near_kernel, (whole, pltpu.HBM((blocks, cout, xs), BF16)), scratch(s...  4.1 us
    pallas_call x1, Pallas kernels, shards(): call(far_kernel, whole, scratch(1), grid=(1,), in_specs=(VMEM, VMEM, VMEM...  4 us
  transfers between devices with their start and end apart: 4, of which 2 were waited for; matrix products, arithmetic and copies ran while one was open for 3% of the time, Pallas kernels for 19%

profile of v5, /device:TPU:3, one launch (start us, length us, event | category | flops | bytes accessed | tf_op | source)
XLA Modules:
  0.0 89.9 jit_solution(1854905299110968626)
XLA Ops:
  0.6 0.0 copy-start
  0.6 0.0 copy-start.2
  0.7 3.3 %shard_map.58 = (bf16[16,2,64,128]{3,2,1,0:T(8,128)(2,1)}, bf16[32,64,128]{2,1,0:T(8,128)(2,1)}) custom-call(bf16[4096,64]{1,0:T(8,128)(2,1)} %bitcast.22, bf16[32,4,64,128]{3,2,1,0:T(8,128)(2,1)} %bitcast.15), custom_call_target="tpu_custom_call" | custom-call | tf_op jit(solution)/shard_map/pallas_call | solution.py:357
  4.0 6.6 %all-to-all-start = ((bf16[16,2,64,128]{3,2,1,0:T(8,128)(2,1)}), bf16[16,2,64,128]{3,2,1,0:T(8,128)(2,1)S(1)}, u32[]{:S(2)}, u32[]{:S(2)}) async-start(bf16[16,2,64,128]{3,2,1,0:T(8,128)(2,1)} %get-tuple-element.9), calls=%async_computation | async-start | bytes 1048576 | tf_op jit(solution)/shard_map/all_to_all | solution.py:377
  10.6 3.4 %collective-permute-start = (bf16[32,64,128]{2,1,0:T(8,128)(2,1)}, bf16[32,64,128]{2,1,0:T(8,128)(2,1)S(1)}, u32[]{:S(2)}, u32[]{:S(2)}) collective-permute-start(bf16[32,64,128]{2,1,0:T(8,128)(2,1)} %get-tuple-element.10), channel_id=1, source_target_pairs={{0,1},{1,2},{2,3},{3,4},{4,5},{5,6},{6,7},{7,8},{8,9},{9,10},{10,1... | collective-permute-start | bytes 1572872 | tf_op jit(solution)/shard_map/ppermute | solution.py:376
  14.0 12.2 %collective-permute-done.halo_ref = bf16[32,64,128]{2,1,0:T(8,128)(2,1)S(1)} collective-permute-done((bf16[32,64,128]{2,1,0:T(8,128)(2,1)}, bf16[32,64,128]{2,1,0:T(8,128)(2,1)S(1)}, u32[]{:S(2)}, u32[]{:S(2)}) %collective-permute-start) | collective-permute-done | bytes 524320 | tf_op jit(solution)/shard_map/ppermute | solution.py:376
  26.2 0.0 copy-done
  26.2 0.0 copy-done.2
  26.2 8.6 %shard_map.59 = (bf16[5,192,2048]{2,1,0:T(8,128)(2,1)}, bf16[16,160,128]{2,1,0:T(8,128)(2,1)}) custom-call(bf16[32,4,64,128]{3,2,1,0:T(8,128)(2,1)S(1)} %bitcast.16, bf16[32,64,128]{2,1,0:T(8,128)(2,1)S(1)} %collective-permute-done.halo_ref, bf16[27,32,64]{2,1,0:T(8,128)(2,1)S(1)} %bitcast.17), custom_call_target="tpu_custom_call" | custom-call | tf_op jit(solution)/shard_map/pallas_call | solution.py:381
  34.8 0.0 all-to-all-done.recv_ref
  34.8 0.0 copy-start.1
  34.8 2.1 %copy-done.1 = bf16[5,192,2048]{2,1,0:T(8,128)(2,1)S(1)} copy-done((bf16[5,192,2048]{2,1,0:T(8,128)(2,1)S(1)}, bf16[5,192,2048]{2,1,0:T(8,128)(2,1)}, u32[]{:S(2)}) %copy-start.1) | copy-done | bytes 3932184
  36.9 2.5 %shard_map.60 = bf16[16,160,128]{2,1,0:T(8,128)(2,1)} custom-call(bf16[16,2,64,128]{3,2,1,0:T(8,128)(2,1)S(1)} %all-to-all-done.recv_ref, bf16[5,192,2048]{2,1,0:T(8,128)(2,1)S(1)} %copy-done.1, bf16[16,160,128]{2,1,0:T(8,128)(2,1)} %get-tuple-element.12.mix_in_ref), custom_call_target="tpu_custom_call", output_to_operand_aliasing={{}: (2, {})} | custom-call | tf_op jit(solution)/shard_map/pallas_call | solution.py:396
  39.4 25.3 %all_to_all.15.back_ref = bf16[16,160,128]{2,1,0:T(8,128)(2,1)S(1)} all-to-all(bf16[16,160,128]{2,1,0:T(8,128)(2,1)} %shard_map.60), channel_id=1, replica_groups=mesh['vol'=2,'gz'=16] {'gz'}, dimensions={0} | all-to-all | bytes 1310720 | tf_op jit(solution)/shard_map/all_to_all | solution.py:414
  64.7 0.7 shard_map.63
  65.4 4.1 %all-to-all-start.2 = ((bf16[32,32,128]{2,1,0:T(8,128)(2,1)}), bf16[32,32,128]{2,1,0:T(8,128)(2,1)S(1)}, u32[]{:S(2)}, u32[]{:S(2)}) async-start(bf16[32,32,128]{2,1,0:T(8,128)(2,1)} %shard_map.63), calls=%async_computation.2 | async-start | bytes 524288 | tf_op jit(solution)/shard_map/all_to_all | solution.py:421
  69.6 4.1 %shard_map.61 = (bf16[32,4,64,128]{3,2,1,0:T(8,128)(2,1)}, bf16[16,64,128]{2,1,0:T(8,128)(2,1)}) custom-call(bf16[16,2,64,128]{3,2,1,0:T(8,128)(2,1)S(1)} %all-to-all-done.recv_ref, bf16[27,32,64]{2,1,0:T(8,128)(2,1)S(1)} %bitcast.18), custom_call_target="tpu_custom_call" | custom-call | tf_op jit(solution)/shard_map/pallas_call | solution.py:433
  73.7 2.5 %collective-permute-start.1 = (bf16[16,64,128]{2,1,0:T(8,128)(2,1)}, bf16[16,64,128]{2,1,0:T(8,128)(2,1)S(1)}, u32[]{:S(2)}, u32[]{:S(2)}) collective-permute-start(bf16[16,64,128]{2,1,0:T(8,128)(2,1)} %get-tuple-element.13), channel_id=1, source_target_pairs={{1,0},{2,1},{3,2},{4,3},{5,4},{6,5},{7,6},{8,7},{9,8},{10,9},{11,1... | collective-permute-start | bytes 786440 | tf_op jit(solution)/shard_map/ppermute | solution.py:444
  76.1 6.3 %collective-permute-done.1.halo_ref = bf16[16,64,128]{2,1,0:T(8,128)(2,1)S(1)} collective-permute-done((bf16[16,64,128]{2,1,0:T(8,128)(2,1)}, bf16[16,64,128]{2,1,0:T(8,128)(2,1)S(1)}, u32[]{:S(2)}, u32[]{:S(2)}) %collective-permute-start.1) | collective-permute-done | bytes 262176 | tf_op jit(solution)/shard_map/ppermute | solution.py:444
  82.4 4.0 %shard_map.62 = bf16[32,4,64,128]{3,2,1,0:T(8,128)(2,1)} custom-call(bf16[16,2,64,128]{3,2,1,0:T(8,128)(2,1)S(1)} %all-to-all-done.recv_ref, bf16[16,64,128]{2,1,0:T(8,128)(2,1)S(1)} %collective-permute-done.1.halo_ref, bf16[27,32,64]{2,1,0:T(8,128)(2,1)S(1)} %bitcast.19, ...), custom_call_target="tpu_custom_call", output_to_operand_aliasing={{}: (3, {})} | custom-call | tf_op jit(solution)/shard_map/pallas_call | solution.py:445
  86.5 0.4 reshape.23
  86.9 2.1 %copy.10 = bf16[32,64,2,64]{3,2,0,1:T(2,128)(2,1)} copy(bf16[32,64,2,64]{3,2,1,0:T(2,128)(2,1)S(1)} %reshape.23) | data formatting | bytes 1048576 | tf_op jit(solution)/shard_map/reshape | solution.py:422
  89.0 0.0 all-to-all-done.2
  89.0 0.9 shard_map.64
  (1 shorter events, 0.0 us)
Async XLA Ops:
  0.6 25.5 %copy-start = (bf16[1,32,4,64,128]{4,3,2,1,0:T(8,128)(2,1)S(1)}, bf16[1,32,4,64,128]{4,3,2,1,0:T(8,128)(2,1)}, u32[]{:S(2)}) copy-start(bf16[1,32,4,64,128]{4,3,2,1,0:T(8,128)(2,1)} %param.3) | copy-start | bytes 6291460
  0.6 25.5 %copy-start.2 = (bf16[64,32,3,3,3]{0,1,4,3,2:T(8,128)(2,1)S(1)}, bf16[64,32,3,3,3]{0,1,4,3,2:T(8,128)(2,1)}, u32[]{:S(2)}) copy-start(bf16[64,32,3,3,3]{0,1,4,3,2:T(8,128)(2,1)} %param.4) | copy-start | bytes 331780
  4.0 30.8 %all-to-all-start = ((bf16[16,2,64,128]{3,2,1,0:T(8,128)(2,1)}), bf16[16,2,64,128]{3,2,1,0:T(8,128)(2,1)S(1)}, u32[]{:S(2)}, u32[]{:S(2)}) async-start(bf16[16,2,64,128]{3,2,1,0:T(8,128)(2,1)} %get-tuple-element.9), calls=%async_computation | async-start | bytes 1048576 | tf_op jit(solution)/shard_map/all_to_all | solution.py:377
  10.6 15.5 %collective-permute-start = (bf16[32,64,128]{2,1,0:T(8,128)(2,1)}, bf16[32,64,128]{2,1,0:T(8,128)(2,1)S(1)}, u32[]{:S(2)}, u32[]{:S(2)}) collective-permute-start(bf16[32,64,128]{2,1,0:T(8,128)(2,1)} %get-tuple-element.10), channel_id=1, source_target_pairs={{0,1},{1,2},{2,3},{3,4},{4,5},{5,6},{6,7},{7,8},{8,9},{9,10},{10,1... | collective-permute-start | bytes 1572872 | tf_op jit(solution)/shard_map/ppermute | solution.py:376
  34.8 2.1 %copy-start.1 = (bf16[5,192,2048]{2,1,0:T(8,128)(2,1)S(1)}, bf16[5,192,2048]{2,1,0:T(8,128)(2,1)}, u32[]{:S(2)}) copy-start(bf16[5,192,2048]{2,1,0:T(8,128)(2,1)} %get-tuple-element.11.xx_ref) | copy-start | bytes 11796484
  65.4 23.6 %all-to-all-start.2 = ((bf16[32,32,128]{2,1,0:T(8,128)(2,1)}), bf16[32,32,128]{2,1,0:T(8,128)(2,1)S(1)}, u32[]{:S(2)}, u32[]{:S(2)}) async-start(bf16[32,32,128]{2,1,0:T(8,128)(2,1)} %shard_map.63), calls=%async_computation.2 | async-start | bytes 524288 | tf_op jit(solution)/shard_map/all_to_all | solution.py:421
  73.7 8.8 %collective-permute-start.1 = (bf16[16,64,128]{2,1,0:T(8,128)(2,1)}, bf16[16,64,128]{2,1,0:T(8,128)(2,1)S(1)}, u32[]{:S(2)}, u32[]{:S(2)}) collective-permute-start(bf16[16,64,128]{2,1,0:T(8,128)(2,1)} %get-tuple-element.13), channel_id=1, source_target_pairs={{1,0},{2,1},{3,2},{4,3},{5,4},{6,5},{7,6},{8,7},{9,8},{10,9},{11,1... | collective-permute-start | bytes 786440 | tf_op jit(solution)/shard_map/ppermute | solution.py:444

commit v6 on v5

--- a/solution.py
+++ b/solution.py
@@ -62,7 +62,7 @@
     return jnp.concatenate([k_ref[at + 2], k_ref[at]], axis=1)
 
 
-def pack_kernel(cot_ref, vol_ref, sent_ref, plane_ref, c_ref, s_ref, packed_ref, v_ref, sems):
+def pack_kernel(cot_ref, vol_ref, sent_ref, plane_ref, c_ref, s_ref, m_ref, packed_ref, v_ref, sems):
     parts = c_ref.shape[0]
     take = pltpu.make_async_copy(vol_ref.at[:, vol_ref.shape[1] - 1], v_ref, sems.at[parts])
     give = pltpu.make_async_copy(v_ref, plane_ref, sems.at[parts + 1])
@@ -78,7 +78,7 @@
     half = cot_ref.shape[1]
     own = cout // parts
     stride = size // own
-    left = iota((own, xs), 1) < half
+    left = iota((size // 2, xs), 1) < half
     leaves = [
         pltpu.make_async_copy(
             packed_ref.at[:, :, pl.ds(i * own, own)],
@@ -90,10 +90,11 @@
     for i in range(parts):
         loads[i].wait()
         s_ref[:, :half] = c_ref[i].astype(F32)
+        low = s_ref[pl.ds(0, size // 2, stride=2), :]
+        high = s_ref[pl.ds(1, size // 2, stride=2), :]
+        m_ref[...] = jnp.where(left, low, pltpu.roll(high, half, axis=1))
         for p in range(count * slots):
-            low = s_ref[pl.ds(2 * p, own, stride=stride), :]
-            high = s_ref[pl.ds(2 * p + 1, own, stride=stride), :]
-            both = jnp.where(left, low, pltpu.roll(high, half, axis=1))
+            both = m_ref[pl.ds(p, own, stride=stride // 2), :]
             packed_ref[p // slots, p % slots, pl.ds(i * own, own)] = both.astype(BF16)
         leaves[i].start()
         if i == 0:
@@ -363,6 +364,7 @@
             (
                 pltpu.VMEM((4, cout * ozs * band // 4, oxs), BF16),
                 pltpu.VMEM((cout * ozs * band // 4, xs), F32),
+                pltpu.VMEM((cout * ozs * band // 8, xs), F32),
                 pltpu.VMEM((count, slots, cout, xs), BF16),
                 pltpu.VMEM((cin, ys, xs), BF16),
                 pltpu.SemaphoreType.DMA((10,)),

time: 90.4 us -> 90.3 us (level)
  no operation moved by 1% of the time
where the time goes in v6:
time: 90.3 us; the launch traced here: 89.8 us
  blocking collectives  25.3 us (28%)
  Pallas kernels  24 us (27%)
  waiting for transfers between devices  18.5 us (20%)
  starting transfers between devices  16.6 us (18%)
  local copies, waits for them, and re-layouts  4.7 us (5%)
    all_to_all x1, blocking collectives, shards(): back = lax.all_to_all(mix, 'gz', 0, 0, tiled=True)  25.3 us
    ppermute x1, waiting for transfers between devices, shards(): under = lax.ppermute(plane, 'gz', [(i, i + 1) for i in range(count - 1)])  12.2 us
    pallas_call x1, Pallas kernels, shards(): call(forward_kernel, (pltpu.HBM((planes + 1, 6 * cin, lanes), BF16), pltp...  8.6 us
    all_to_all x1, starting transfers between devices, shards(): recv = lax.all_to_all(packed, 'gz', 0, 0, tiled=True)  6.65 us
    ppermute x1, waiting for transfers between devices, shards(): above = lax.ppermute(edge, 'gz', [(i + 1, i) for i in range(count - 1)])  6.32 us
    all_to_all x1, starting transfers between devices, shards(): total = lax.all_to_all(total, ('vol', 'gz'), 0, 0, tiled=True)  4.15 us
    pallas_call x1, Pallas kernels, shards(): call(near_kernel, (whole, pltpu.HBM((blocks, cout, xs), BF16)), scratch(s...  4.1 us
    pallas_call x1, Pallas kernels, shards(): call(far_kernel, whole, scratch(1), grid=(1,), in_specs=(VMEM, VMEM, VMEM...  4 us
  transfers between devices with their start and end apart: 4, of which 2 were waited for; matrix products, arithmetic and copies ran while one was open for 3% of the time, Pallas kernels for 19%

profile of v6, /device:TPU:3, one launch (start us, length us, event | category | flops | bytes accessed | tf_op | source)
XLA Modules:
  0.0 89.8 jit_solution(8799669449044608459)
XLA Ops:
  0.6 0.0 copy-start
  0.6 0.0 copy-start.2
  0.7 3.2 %shard_map.58 = (bf16[16,2,64,128]{3,2,1,0:T(8,128)(2,1)}, bf16[32,64,128]{2,1,0:T(8,128)(2,1)}) custom-call(bf16[4096,64]{1,0:T(8,128)(2,1)} %bitcast.22, bf16[32,4,64,128]{3,2,1,0:T(8,128)(2,1)} %bitcast.15), custom_call_target="tpu_custom_call" | custom-call | tf_op jit(solution)/shard_map/pallas_call | solution.py:358
  3.9 6.6 %all-to-all-start = ((bf16[16,2,64,128]{3,2,1,0:T(8,128)(2,1)}), bf16[16,2,64,128]{3,2,1,0:T(8,128)(2,1)S(1)}, u32[]{:S(2)}, u32[]{:S(2)}) async-start(bf16[16,2,64,128]{3,2,1,0:T(8,128)(2,1)} %get-tuple-element.9), calls=%async_computation | async-start | bytes 1048576 | tf_op jit(solution)/shard_map/all_to_all | solution.py:379
  10.5 3.4 %collective-permute-start = (bf16[32,64,128]{2,1,0:T(8,128)(2,1)}, bf16[32,64,128]{2,1,0:T(8,128)(2,1)S(1)}, u32[]{:S(2)}, u32[]{:S(2)}) collective-permute-start(bf16[32,64,128]{2,1,0:T(8,128)(2,1)} %get-tuple-element.10), channel_id=1, source_target_pairs={{0,1},{1,2},{2,3},{3,4},{4,5},{5,6},{6,7},{7,8},{8,9},{9,10},{10,1... | collective-permute-start | bytes 1572872 | tf_op jit(solution)/shard_map/ppermute | solution.py:378
  13.9 12.2 %collective-permute-done.halo_ref = bf16[32,64,128]{2,1,0:T(8,128)(2,1)S(1)} collective-permute-done((bf16[32,64,128]{2,1,0:T(8,128)(2,1)}, bf16[32,64,128]{2,1,0:T(8,128)(2,1)S(1)}, u32[]{:S(2)}, u32[]{:S(2)}) %collective-permute-start) | collective-permute-done | bytes 524320 | tf_op jit(solution)/shard_map/ppermute | solution.py:378
  26.1 0.0 copy-done
  26.1 0.0 copy-done.2
  26.1 8.6 %shard_map.59 = (bf16[5,192,2048]{2,1,0:T(8,128)(2,1)}, bf16[16,160,128]{2,1,0:T(8,128)(2,1)}) custom-call(bf16[32,4,64,128]{3,2,1,0:T(8,128)(2,1)S(1)} %bitcast.16, bf16[32,64,128]{2,1,0:T(8,128)(2,1)S(1)} %collective-permute-done.halo_ref, bf16[27,32,64]{2,1,0:T(8,128)(2,1)S(1)} %bitcast.17), custom_call_target="tpu_custom_call" | custom-call | tf_op jit(solution)/shard_map/pallas_call | solution.py:383
  34.7 0.0 all-to-all-done.recv_ref
  34.7 0.0 copy-start.1
  34.7 2.1 %copy-done.1 = bf16[5,192,2048]{2,1,0:T(8,128)(2,1)S(1)} copy-done((bf16[5,192,2048]{2,1,0:T(8,128)(2,1)S(1)}, bf16[5,192,2048]{2,1,0:T(8,128)(2,1)}, u32[]{:S(2)}) %copy-start.1) | copy-done | bytes 3932184
  36.8 2.5 %shard_map.60 = bf16[16,160,128]{2,1,0:T(8,128)(2,1)} custom-call(bf16[16,2,64,128]{3,2,1,0:T(8,128)(2,1)S(1)} %all-to-all-done.recv_ref, bf16[5,192,2048]{2,1,0:T(8,128)(2,1)S(1)} %copy-done.1, bf16[16,160,128]{2,1,0:T(8,128)(2,1)} %get-tuple-element.12.mix_in_ref), custom_call_target="tpu_custom_call", output_to_operand_aliasing={{}: (2, {})} | custom-call | tf_op jit(solution)/shard_map/pallas_call | solution.py:398
  39.3 25.3 %all_to_all.15.back_ref = bf16[16,160,128]{2,1,0:T(8,128)(2,1)S(1)} all-to-all(bf16[16,160,128]{2,1,0:T(8,128)(2,1)} %shard_map.60), channel_id=1, replica_groups=mesh['vol'=2,'gz'=16] {'gz'}, dimensions={0} | all-to-all | bytes 1310720 | tf_op jit(solution)/shard_map/all_to_all | solution.py:416
  64.6 0.7 shard_map.63
  65.3 4.1 %all-to-all-start.2 = ((bf16[32,32,128]{2,1,0:T(8,128)(2,1)}), bf16[32,32,128]{2,1,0:T(8,128)(2,1)S(1)}, u32[]{:S(2)}, u32[]{:S(2)}) async-start(bf16[32,32,128]{2,1,0:T(8,128)(2,1)} %shard_map.63), calls=%async_computation.2 | async-start | bytes 524288 | tf_op jit(solution)/shard_map/all_to_all | solution.py:423
  69.5 4.1 %shard_map.61 = (bf16[32,4,64,128]{3,2,1,0:T(8,128)(2,1)}, bf16[16,64,128]{2,1,0:T(8,128)(2,1)}) custom-call(bf16[16,2,64,128]{3,2,1,0:T(8,128)(2,1)S(1)} %all-to-all-done.recv_ref, bf16[27,32,64]{2,1,0:T(8,128)(2,1)S(1)} %bitcast.18), custom_call_target="tpu_custom_call" | custom-call | tf_op jit(solution)/shard_map/pallas_call | solution.py:435
  73.6 2.5 %collective-permute-start.1 = (bf16[16,64,128]{2,1,0:T(8,128)(2,1)}, bf16[16,64,128]{2,1,0:T(8,128)(2,1)S(1)}, u32[]{:S(2)}, u32[]{:S(2)}) collective-permute-start(bf16[16,64,128]{2,1,0:T(8,128)(2,1)} %get-tuple-element.13), channel_id=1, source_target_pairs={{1,0},{2,1},{3,2},{4,3},{5,4},{6,5},{7,6},{8,7},{9,8},{10,9},{11,1... | collective-permute-start | bytes 786440 | tf_op jit(solution)/shard_map/ppermute | solution.py:446
  76.0 6.3 %collective-permute-done.1.halo_ref = bf16[16,64,128]{2,1,0:T(8,128)(2,1)S(1)} collective-permute-done((bf16[16,64,128]{2,1,0:T(8,128)(2,1)}, bf16[16,64,128]{2,1,0:T(8,128)(2,1)S(1)}, u32[]{:S(2)}, u32[]{:S(2)}) %collective-permute-start.1) | collective-permute-done | bytes 262176 | tf_op jit(solution)/shard_map/ppermute | solution.py:446
  82.3 4.0 %shard_map.62 = bf16[32,4,64,128]{3,2,1,0:T(8,128)(2,1)} custom-call(bf16[16,2,64,128]{3,2,1,0:T(8,128)(2,1)S(1)} %all-to-all-done.recv_ref, bf16[16,64,128]{2,1,0:T(8,128)(2,1)S(1)} %collective-permute-done.1.halo_ref, bf16[27,32,64]{2,1,0:T(8,128)(2,1)S(1)} %bitcast.19, ...), custom_call_target="tpu_custom_call", output_to_operand_aliasing={{}: (3, {})} | custom-call | tf_op jit(solution)/shard_map/pallas_call | solution.py:447
  86.4 0.4 reshape.23
  86.8 2.1 %copy.10 = bf16[32,64,2,64]{3,2,0,1:T(2,128)(2,1)} copy(bf16[32,64,2,64]{3,2,1,0:T(2,128)(2,1)S(1)} %reshape.23) | data formatting | bytes 1048576 | tf_op jit(solution)/shard_map/reshape | solution.py:424
  88.9 0.0 all-to-all-done.2
  88.9 0.9 shard_map.64
  (1 shorter events, 0.0 us)
Async XLA Ops:
  0.6 25.4 %copy-start = (bf16[1,32,4,64,128]{4,3,2,1,0:T(8,128)(2,1)S(1)}, bf16[1,32,4,64,128]{4,3,2,1,0:T(8,128)(2,1)}, u32[]{:S(2)}) copy-start(bf16[1,32,4,64,128]{4,3,2,1,0:T(8,128)(2,1)} %param.3) | copy-start | bytes 6291460
  0.6 25.4 %copy-start.2 = (bf16[64,32,3,3,3]{0,1,4,3,2:T(8,128)(2,1)S(1)}, bf16[64,32,3,3,3]{0,1,4,3,2:T(8,128)(2,1)}, u32[]{:S(2)}) copy-start(bf16[64,32,3,3,3]{0,1,4,3,2:T(8,128)(2,1)} %param.4) | copy-start | bytes 331780
  3.9 30.8 %all-to-all-start = ((bf16[16,2,64,128]{3,2,1,0:T(8,128)(2,1)}), bf16[16,2,64,128]{3,2,1,0:T(8,128)(2,1)S(1)}, u32[]{:S(2)}, u32[]{:S(2)}) async-start(bf16[16,2,64,128]{3,2,1,0:T(8,128)(2,1)} %get-tuple-element.9), calls=%async_computation | async-start | bytes 1048576 | tf_op jit(solution)/shard_map/all_to_all | solution.py:379
  10.5 15.5 %collective-permute-start = (bf16[32,64,128]{2,1,0:T(8,128)(2,1)}, bf16[32,64,128]{2,1,0:T(8,128)(2,1)S(1)}, u32[]{:S(2)}, u32[]{:S(2)}) collective-permute-start(bf16[32,64,128]{2,1,0:T(8,128)(2,1)} %get-tuple-element.10), channel_id=1, source_target_pairs={{0,1},{1,2},{2,3},{3,4},{4,5},{5,6},{6,7},{7,8},{8,9},{9,10},{10,1... | collective-permute-start | bytes 1572872 | tf_op jit(solution)/shard_map/ppermute | solution.py:378
  34.7 2.1 %copy-start.1 = (bf16[5,192,2048]{2,1,0:T(8,128)(2,1)S(1)}, bf16[5,192,2048]{2,1,0:T(8,128)(2,1)}, u32[]{:S(2)}) copy-start(bf16[5,192,2048]{2,1,0:T(8,128)(2,1)} %get-tuple-element.11.xx_ref) | copy-start | bytes 11796484
  65.3 23.7 %all-to-all-start.2 = ((bf16[32,32,128]{2,1,0:T(8,128)(2,1)}), bf16[32,32,128]{2,1,0:T(8,128)(2,1)S(1)}, u32[]{:S(2)}, u32[]{:S(2)}) async-start(bf16[32,32,128]{2,1,0:T(8,128)(2,1)} %shard_map.63), calls=%async_computation.2 | async-start | bytes 524288 | tf_op jit(solution)/shard_map/all_to_all | solution.py:423
  73.6 8.8 %collective-permute-start.1 = (bf16[16,64,128]{2,1,0:T(8,128)(2,1)}, bf16[16,64,128]{2,1,0:T(8,128)(2,1)S(1)}, u32[]{:S(2)}, u32[]{:S(2)}) collective-permute-start(bf16[16,64,128]{2,1,0:T(8,128)(2,1)} %get-tuple-element.13), channel_id=1, source_target_pairs={{1,0},{2,1},{3,2},{4,3},{5,4},{6,5},{7,6},{8,7},{9,8},{10,9},{11,1... | collective-permute-start | bytes 786440 | tf_op jit(solution)/shard_map/ppermute | solution.py:446
